TPU v7x, 256 devices: a whole 4x4x8 slice. The times are simulated.
256 devices in a mesh: ctx: 32 (over z, y), head: 8 (over x, core).
Axes of the slice: x: 4, y: 4, z: 8, core: 2. Of those that a mesh axis runs over, the one named last changes fastest.
Arguments:
- queries: bfloat16 [32, 512, 3072], P('ctx', None, 'head'), may hold values from -5 to 5
- key_rows: bfloat16 [32, 512, 3072], P('ctx', None, 'head'), may hold values from -5 to 5
- value_rows: bfloat16 [32, 512, 3072], P('ctx', None, 'head'), may hold values from -6 to 6
- out_grad: bfloat16 [32, 512, 3072], P('ctx', None, 'head'), may hold values from -6 to 6
- head_kind: int32 [24], replicated, may hold values from 0 to 1, as said below
- frame_band: int32 [24], replicated, may hold values from 1 to 31, as said below
Outputs:
- attended: bfloat16 [32, 512, 3072], P('ctx', None, 'head')
- query_grad: bfloat16 [32, 512, 3072], P('ctx', None, 'head')
- key_grad: bfloat16 [32, 512, 3072], P('ctx', None, 'head')
- value_grad: bfloat16 [32, 512, 3072], P('ctx', None, 'head')
Inputs may be any that keep to these rules, and one draw needn't show every extreme that they name: `head_kind`: exactly 8 entries are 1. `frame_band`: entries of spatial heads are not used; some temporal head has the value 32 - 1.
All inputs are finite; a program needn't handle non-finite values.
Results may differ from a plain program's by a relative error of at most 0.024.
Values may be sent and summed in bfloat16 or wider, within the bound.
A program may use at most 64 MiB of HBM per device.

v0:
```python
import jax
import jax.numpy as jnp
from jax import lax
from jax.sharding import PartitionSpec as P

DH = 128


def passed_along(array, axis, by):
    length = lax.axis_size(axis)
    pairs = [(i, i + by) for i in range(length) if 0 <= i + by < length]
    return lax.ppermute(array, axis, pairs)


def for_sending(array):

    def short(part):
        return part.astype(jnp.bfloat16) if part.dtype == jnp.float32 else part

    return jax.tree.map(short, array)


def log_sum(scores):
    top_value = jnp.max(scores, axis=-1, keepdims=True)
    return top_value + jnp.log(jnp.sum(jnp.exp(scores - top_value), axis=-1, keepdims=True))


def spatial_head(q_head, k_head, v_head, g_head, k_prior, v_prior, has_prior):
    count = q_head.shape[0]
    scaling = DH ** (-0.5)
    key_pair = jnp.concatenate([k_prior, k_head], axis=0)
    value_pair = jnp.concatenate([v_prior, v_head], axis=0)
    valid = jnp.concatenate(
        [jnp.broadcast_to(has_prior, (count,)), jnp.ones((count,), dtype=bool)]
    )[None, :]
    out_parts, grad_parts, lse_parts, delta_parts = ([], [], [], [])
    score = jnp.einsum("qd,kd->qk", q_head, key_pair, preferred_element_type=jnp.float32) * scaling
    score = jnp.where(valid, score, -jnp.inf)
    lse_part = log_sum(score)
    weight = jnp.exp(score - lse_part)
    prob = weight.astype(jnp.bfloat16)
    attended = jnp.dot(prob, value_pair, preferred_element_type=jnp.float32).astype(jnp.bfloat16)
    delta = jnp.sum(
        g_head.astype(jnp.float32) * attended.astype(jnp.float32), axis=-1, keepdims=True
    )
    dprob = jnp.einsum("qd,kd->qk", g_head, value_pair, preferred_element_type=jnp.float32)
    dscore = (weight * (dprob - delta) * scaling).astype(jnp.bfloat16)
    grad_parts.append(
        jnp.dot(dscore, key_pair, preferred_element_type=jnp.float32).astype(jnp.bfloat16)
    )
    k_total = jnp.einsum("qk,qd->kd", dscore, q_head, preferred_element_type=jnp.float32)
    v_total = jnp.einsum("qk,qd->kd", prob, g_head, preferred_element_type=jnp.float32)
    out_parts.append(attended)
    lse_parts.append(lse_part[:, 0])
    delta_parts.append(delta[:, 0])
    return (
        jnp.concatenate(out_parts, axis=0),
        jnp.concatenate(grad_parts, axis=0),
        k_total,
        v_total,
        jnp.concatenate(lse_parts, axis=0),
        jnp.concatenate(delta_parts, axis=0),
    )


def blank_spatial(count):
    key_count = 2 * count
    return (
        jnp.zeros((count, DH), jnp.bfloat16),
        jnp.zeros((count, DH), jnp.bfloat16),
        jnp.zeros((key_count, DH), jnp.float32),
        jnp.zeros((key_count, DH), jnp.float32),
        jnp.zeros((count,), jnp.float32),
        jnp.zeros((count,), jnp.float32),
    )


def temporal_heads(t_query, t_key, t_value, t_grad, band_heads):
    scaling = DH ** (-0.5)
    frame_total = t_query.shape[0]
    score = (
        jnp.einsum("frtd,grtd->rtfg", t_query, t_key, preferred_element_type=jnp.float32) * scaling
    )
    frame_ids = jnp.arange(frame_total, dtype=jnp.int32)
    distance = jnp.abs(frame_ids[:, None] - frame_ids[None, :])
    allowed = distance[None, None, :, :] <= band_heads[None, :, None, None]
    score = jnp.where(allowed, score, -jnp.inf)
    weight = jnp.exp(score - log_sum(score))
    prob = weight.astype(jnp.bfloat16)
    attended = jnp.einsum(
        "rtfg,grtd->frtd", prob, t_value, preferred_element_type=jnp.float32
    ).astype(jnp.bfloat16)
    delta = jnp.sum(t_grad.astype(jnp.float32) * attended.astype(jnp.float32), axis=-1)
    delta = jnp.transpose(delta, (1, 2, 0))[..., None]
    dprob = jnp.einsum("frtd,grtd->rtfg", t_grad, t_value, preferred_element_type=jnp.float32)
    dscore = (weight * (dprob - delta) * scaling).astype(jnp.bfloat16)
    q_grad = jnp.einsum(
        "rtfg,grtd->frtd", dscore, t_key, preferred_element_type=jnp.float32
    ).astype(jnp.bfloat16)
    k_grad = jnp.einsum(
        "rtfg,frtd->grtd", dscore, t_query, preferred_element_type=jnp.float32
    ).astype(jnp.bfloat16)
    v_grad = jnp.einsum("rtfg,frtd->grtd", prob, t_grad, preferred_element_type=jnp.float32).astype(
        jnp.bfloat16
    )
    return (attended, q_grad, k_grad, v_grad)


def body(queries, key_rows, value_rows, out_grad, head_kind, frame_band):
    count = queries.shape[1]
    local_heads = queries.shape[2] // DH
    head_place = lax.axis_index("head")
    frame = lax.axis_index("ctx")
    local_kind = lax.dynamic_slice_in_dim(head_kind, head_place * local_heads, local_heads)
    q_local = queries[0]
    k_local = key_rows[0]
    v_local = value_rows[0]
    g_local = out_grad[0]
    k_prior, v_prior = passed_along((k_local, v_local), "ctx", 1)
    outcome = []
    for column in range(local_heads):
        head_cols = slice(column * DH, (column + 1) * DH)

        def run_spatial(cols=head_cols):
            return spatial_head(
                q_local[:, cols],
                k_local[:, cols],
                v_local[:, cols],
                g_local[:, cols],
                k_prior[:, cols],
                v_prior[:, cols],
                frame > 0,
            )

        def run_blank():
            return blank_spatial(count)

        outcome.append(lax.cond(local_kind[column] == 1, run_spatial, run_blank))
    k_send = jnp.concatenate([item[2][:count] for item in outcome], axis=1)
    v_send = jnp.concatenate([item[3][:count] for item in outcome], axis=1)
    k_own = jnp.concatenate([item[2][count:] for item in outcome], axis=1)
    v_own = jnp.concatenate([item[3][count:] for item in outcome], axis=1)
    k_back, v_back = (
        passed_along(k_send.astype(jnp.bfloat16), "ctx", -1).astype(k_send.dtype),
        passed_along(v_send.astype(jnp.bfloat16), "ctx", -1).astype(v_send.dtype),
    )
    k_spatial = k_own + k_back
    v_spatial = v_own + v_back
    out_spatial = jnp.concatenate([item[0] for item in outcome], axis=1)
    qgrad_spatial = jnp.concatenate([item[1] for item in outcome], axis=1)
    local_band = lax.dynamic_slice_in_dim(frame_band, head_place * local_heads, local_heads)
    local_rows = tuple(
        (x.reshape(1, count, local_heads, DH) for x in (q_local, k_local, v_local, g_local))
    )
    framed = jax.tree.map(
        lambda part, own: part.astype(own.dtype),
        lax.all_to_all(for_sending(local_rows), "ctx", split_axis=1, concat_axis=0, tiled=True),
        local_rows,
    )
    results = temporal_heads(framed[0], framed[1], framed[2], framed[3], local_band)
    returned = (
        lax.all_to_all(results[0], "ctx", split_axis=0, concat_axis=1, tiled=True),
        lax.all_to_all(results[1], "ctx", split_axis=0, concat_axis=1, tiled=True),
        lax.all_to_all(results[2], "ctx", split_axis=0, concat_axis=1, tiled=True),
        lax.all_to_all(results[3], "ctx", split_axis=0, concat_axis=1, tiled=True),
    )
    home_rows = tuple((x[0] for x in returned))
    temporal_flat = tuple((x.reshape(count, local_heads * DH) for x in home_rows))
    spatial_cols = jnp.repeat(local_kind == 1, DH)[None, :]
    attended = jnp.where(spatial_cols, out_spatial, temporal_flat[0])
    query_grad = jnp.where(spatial_cols, qgrad_spatial, temporal_flat[1])
    key_grad = jnp.where(spatial_cols, k_spatial.astype(jnp.bfloat16), temporal_flat[2])
    value_grad = jnp.where(spatial_cols, v_spatial.astype(jnp.bfloat16), temporal_flat[3])
    return (attended[None], query_grad[None], key_grad[None], value_grad[None])


def solution(mesh):
    placed = (
        P("ctx", None, "head"),
        P("ctx", None, "head"),
        P("ctx", None, "head"),
        P("ctx", None, "head"),
        P(),
        P(),
    )
    return jax.shard_map(
        body,
        mesh=mesh,
        in_specs=placed,
        out_specs=(
            P("ctx", None, "head"),
            P("ctx", None, "head"),
            P("ctx", None, "head"),
            P("ctx", None, "head"),
        ),
        check_vma=False,
    )
```

profile of v0, /device:TPU:34, one launch (start us, length us, event | category | flops | bytes accessed | tf_op | source)
XLA Modules:
  0.0 219.9 jit_solution(5006015062498947849)
XLA Ops:
  3.0 11.5 %all-to-all-start = ((bf16[1,512,3,128]{3,2,0,1:T(4,128)(2,1)}), bf16[1,512,3,128]{3,2,0,1:T(4,128)(2,1)S(1)}, u32[]{:S(2)}, u32[]{:S(2)}) async-start(bf16[1,512,3,128]{3,2,0,1:T(4,128)(2,1)} %copy.94), calls=%async_computation | async-start | bytes 1048576 | tf_op jit(solution)/shard_map/all_to_all | solution.py:157
  15.7 15.9 %all-to-all-done = bf16[1,512,3,128]{3,2,0,1:T(4,128)(2,1)S(1)} async-done(((bf16[1,512,3,128]{3,2,0,1:T(4,128)(2,1)}), bf16[1,512,3,128]{3,2,0,1:T(4,128)(2,1)S(1)}, u32[]{:S(2)}, u32[]{:S(2)}) %all-to-all-start) | async-done | bytes 393248 | tf_op jit(solution)/shard_map/all_to_all | solution.py:157
  31.6 5.2 %all-to-all-start.1 = ((bf16[1,512,3,128]{3,2,0,1:T(4,128)(2,1)}), bf16[1,512,3,128]{3,2,0,1:T(4,128)(2,1)S(1)}, u32[]{:S(2)}, u32[]{:S(2)}) async-start(bf16[1,512,3,128]{3,2,0,1:T(4,128)(2,1)} %copy.97), calls=%async_computation.1 | async-start | bytes 1048576 | tf_op jit(solution)/shard_map/all_to_all | solution.py:157
  38.2 15.1 %all-to-all-done.1 = bf16[1,512,3,128]{3,2,0,1:T(4,128)(2,1)S(1)} async-done(((bf16[1,512,3,128]{3,2,0,1:T(4,128)(2,1)}), bf16[1,512,3,128]{3,2,0,1:T(4,128)(2,1)S(1)}, u32[]{:S(2)}, u32[]{:S(2)}) %all-to-all-start.1) | async-done | bytes 393248 | tf_op jit(solution)/shard_map/all_to_all | solution.py:157
  53.2 5.1 %all-to-all-start.4 = ((bf16[1,512,3,128]{3,2,0,1:T(4,128)(2,1)}), bf16[1,512,3,128]{3,2,0,1:T(4,128)(2,1)S(1)}, u32[]{:S(2)}, u32[]{:S(2)}) async-start(bf16[1,512,3,128]{3,2,0,1:T(4,128)(2,1)} %copy.109), calls=%async_computation.4 | async-start | bytes 1048576 | tf_op jit(solution)/shard_map/all_to_all | solution.py:157
  61.4 13.2 %all-to-all-done.4 = bf16[1,512,3,128]{3,2,0,1:T(4,128)(2,1)S(1)} async-done(((bf16[1,512,3,128]{3,2,0,1:T(4,128)(2,1)}), bf16[1,512,3,128]{3,2,0,1:T(4,128)(2,1)S(1)}, u32[]{:S(2)}, u32[]{:S(2)}) %all-to-all-start.4) | async-done | bytes 393248 | tf_op jit(solution)/shard_map/all_to_all | solution.py:157
  74.7 5.1 %all-to-all-start.2 = ((bf16[1,512,3,128]{3,2,0,1:T(4,128)(2,1)}), bf16[1,512,3,128]{3,2,0,1:T(4,128)(2,1)S(1)}, u32[]{:S(2)}, u32[]{:S(2)}) async-start(bf16[1,512,3,128]{3,2,0,1:T(4,128)(2,1)} %copy.102), calls=%async_computation.2 | async-start | bytes 1048576 | tf_op jit(solution)/shard_map/all_to_all | solution.py:157
  79.8 1.5 fusion.71
  82.8 13.3 %all-to-all-done.2 = bf16[1,512,3,128]{3,2,0,1:T(4,128)(2,1)S(1)} async-done(((bf16[1,512,3,128]{3,2,0,1:T(4,128)(2,1)}), bf16[1,512,3,128]{3,2,0,1:T(4,128)(2,1)S(1)}, u32[]{:S(2)}, u32[]{:S(2)}) %all-to-all-start.2) | async-done | bytes 393248 | tf_op jit(solution)/shard_map/all_to_all | solution.py:157
  96.0 5.1 %all-to-all-start.7 = ((bf16[32,16,3,128]{3,1,2,0:T(8,128)(2,1)}), bf16[32,16,3,128]{3,1,2,0:T(8,128)(2,1)S(1)}, u32[]{:S(2)}, u32[]{:S(2)}) async-start(bf16[32,16,3,128]{3,1,2,0:T(8,128)(2,1)} %copy.123), calls=%async_computation.7 | async-start | bytes 786432 | tf_op jit(solution)/shard_map/all_to_all | solution.py:165
  104.4 10.3 %all-to-all-done.7 = bf16[32,16,3,128]{3,1,2,0:T(8,128)(2,1)S(1)} async-done(((bf16[32,16,3,128]{3,1,2,0:T(8,128)(2,1)}), bf16[32,16,3,128]{3,1,2,0:T(8,128)(2,1)S(1)}, u32[]{:S(2)}, u32[]{:S(2)}) %all-to-all-start.7) | async-done | bytes 393248 | tf_op jit(solution)/shard_map/all_to_all | solution.py:165
  114.7 4.9 %all-to-all-start.5 = ((bf16[32,16,3,128]{3,1,2,0:T(8,128)(2,1)}), bf16[32,16,3,128]{3,1,2,0:T(8,128)(2,1)S(1)}, u32[]{:S(2)}, u32[]{:S(2)}) async-start(bf16[32,16,3,128]{3,1,2,0:T(8,128)(2,1)} %copy.117), calls=%async_computation.5 | async-start | bytes 786432 | tf_op jit(solution)/shard_map/all_to_all | solution.py:163
  120.5 12.4 %all-to-all-done.5 = bf16[32,16,3,128]{3,1,2,0:T(8,128)(2,1)S(1)} async-done(((bf16[32,16,3,128]{3,1,2,0:T(8,128)(2,1)}), bf16[32,16,3,128]{3,1,2,0:T(8,128)(2,1)S(1)}, u32[]{:S(2)}, u32[]{:S(2)}) %all-to-all-start.5) | async-done | bytes 393248 | tf_op jit(solution)/shard_map/all_to_all | solution.py:163
  133.0 4.9 %all-to-all-start.3 = ((bf16[32,16,3,128]{3,1,2,0:T(8,128)(2,1)}), bf16[32,16,3,128]{3,1,2,0:T(8,128)(2,1)S(1)}, u32[]{:S(2)}, u32[]{:S(2)}) async-start(bf16[32,16,3,128]{3,1,2,0:T(8,128)(2,1)} %copy.106), calls=%async_computation.3 | async-start | bytes 786432 | tf_op jit(solution)/shard_map/all_to_all | solution.py:162
  137.9 3.4 %collective-permute-start = (bf16[512,384]{1,0:T(8,128)(2,1)S(1)}, bf16[512,384]{1,0:T(8,128)(2,1)}, u32[]{:S(2)}, u32[]{:S(2)}) collective-permute-start(bf16[512,384]{1,0:T(8,128)(2,1)S(1)} %bitcast.64), channel_id=1, source_target_pairs={{0,8},{8,16},{16,24},{24,32},{32,40},{40,48},{48,56},{56,64},{64,7... | collective-permute-start | bytes 1179656 | tf_op jit(solution)/shard_map/ppermute | solution.py:12
  141.3 3.4 %collective-permute-start.1 = (bf16[512,384]{1,0:T(8,128)(2,1)S(1)}, bf16[512,384]{1,0:T(8,128)(2,1)}, u32[]{:S(2)}, u32[]{:S(2)}) collective-permute-start(bf16[512,384]{1,0:T(8,128)(2,1)S(1)} %bitcast.68), channel_id=1, source_target_pairs={{0,8},{8,16},{16,24},{24,32},{32,40},{40,48},{48,56},{56,64},{64,7... | collective-permute-start | bytes 1179656 | tf_op jit(solution)/shard_map/ppermute | solution.py:12
  146.8 4.3 %all-to-all-done.3 = bf16[32,16,3,128]{3,1,2,0:T(8,128)(2,1)S(1)} async-done(((bf16[32,16,3,128]{3,1,2,0:T(8,128)(2,1)}), bf16[32,16,3,128]{3,1,2,0:T(8,128)(2,1)S(1)}, u32[]{:S(2)}, u32[]{:S(2)}) %all-to-all-start.3) | async-done | bytes 393248 | tf_op jit(solution)/shard_map/all_to_all | solution.py:162
  151.1 6.8 %all-to-all-start.6 = ((bf16[32,16,3,128]{3,1,2,0:T(8,128)(2,1)}), bf16[32,16,3,128]{3,1,2,0:T(8,128)(2,1)}, u32[]{:S(2)}, u32[]{:S(2)}) async-start(bf16[32,16,3,128]{3,1,2,0:T(8,128)(2,1)} %copy.120), calls=%async_computation.6 | async-start | bytes 786432 | tf_op jit(solution)/shard_map/all_to_all | solution.py:164
  160.6 9.9 %collective-permute-done.1 = bf16[512,384]{1,0:T(8,128)(2,1)} collective-permute-done((bf16[512,384]{1,0:T(8,128)(2,1)S(1)}, bf16[512,384]{1,0:T(8,128)(2,1)}, u32[]{:S(2)}, u32[]{:S(2)}) %collective-permute-start.1) | collective-permute-done | bytes 393248 | tf_op jit(solution)/shard_map/ppermute | solution.py:12
  170.5 10.0 %conditional.5 = (bf16[1,512,128]{2,1,0:T(8,128)(2,1)S(1)}, f32[512,128]{1,0:T(8,128)S(1)}, f32[512,128]{1,0:T(8,128)S(1)}, bf16[512,128]{1,0:T(8,128)(2,1)S(1)}...) conditional(s32[]{:T(128)} %bitcast.13, () %tuple.71, (s32[]{:T(128)}, ...), branch_computations={%region_10.11_spmd, %region_11.15_spmd} | conditional | flops 815135744 | bytes 21652652 | solution.py:138
  172.7 1.4 fusion.69
  175.6 1.7 copy.133
  181.5 9.8 %conditional.4 = (bf16[1,512,128]{2,1,0:T(8,128)(2,1)S(1)}, f32[512,128]{1,0:T(8,128)S(1)}, f32[512,128]{1,0:T(8,128)S(1)}, bf16[512,128]{1,0:T(8,128)(2,1)S(1)}...) conditional(s32[]{:T(128)} %bitcast.12, () %tuple.70, (s32[]{:T(128)}, bf16[512,384]{1,0:T(8,128)(2,1)}, ...), branch_computations={%region_5.6_spmd, %region_6.10_spmd} | conditional | flops 815135744 | bytes 21652652 | solution.py:138
  183.5 1.4 fusion.68
  186.4 1.7 copy.131
  192.3 9.1 %conditional.3 = (bf16[1,512,128]{2,1,0:T(8,128)(2,1)S(1)}, f32[512,128]{1,0:T(8,128)}, f32[512,128]{1,0:T(8,128)}, bf16[512,128]{1,0:T(8,128)(2,1)S(1)}, bf16[5...) conditional(s32[]{:T(128)} %bitcast.7, () %tuple.68, (s32[]{:T(128)}, bf16[512,384]{1,0:T(8,128)(2,1)}, ...), branch_computations={%region_0.0_spmd, %region_1.5_spmd} | conditional | flops 815135744 | bytes 21652652 | solution.py:138
  201.4 1.8 pad_maximum_fusion.19
  203.2 1.9 collective-permute-start.3
  205.2 1.8 pad_maximum_fusion.18
  207.0 1.9 collective-permute-start.2
  214.0 3.4 %collective-permute-done.2 = bf16[512,384]{1,0:T(8,128)(2,1)} collective-permute-done((bf16[512,384]{1,0:T(8,128)(2,1)}, bf16[512,384]{1,0:T(8,128)(2,1)}, u32[]{:S(2)}, u32[]{:S(2)}) %collective-permute-start.2) | collective-permute-done | bytes 393248 | tf_op jit(solution)/shard_map/ppermute | solution.py:12
  217.4 2.5 %fusion.54 = (bf16[1,512,384]{2,1,0:T(8,128)(2,1)}, bf16[1,512,384]{2,1,0:T(8,128)(2,1)}) fusion(bf16[512,384]{1,0:T(8,128)(2,1)} %collective-permute-done.3, f32[512,128]{1,0:T(8,128)S(1)} %copy-done.13, f32[512,128]{1,0:T(8,128)S(1)} %copy-done.17, f32[512,128]{1,0:T(8,128)} %get-tuple-element.172, bf16[64,8,3,128]{3,2,1,0:T(4,128)(2,1)S(1)} %bitcast.62, ...), kind=kLoop, calls=%fused_computation.95 | loop fusion | flops 2359296 | bytes 3932544 | tf_op jit(solution)/shard_map/broadcast_in_dim | solution.py:174
  (186 shorter events, 45.5 us)
Async XLA Ops:
  0.6 13.8 %copy-start = (bf16[1,512,384]{2,1,0:T(8,128)(2,1)S(1)}, bf16[1,512,384]{2,1,0:T(8,128)(2,1)}, u32[]{:S(2)}) copy-start(bf16[1,512,384]{2,1,0:T(8,128)(2,1)} %param.13) | copy-start | bytes 1179652
  3.0 33.9 %copy-start.32 = (bf16[1,512,384]{2,1,0:T(8,128)(2,1)S(1)}, bf16[1,512,384]{2,1,0:T(8,128)(2,1)}, u32[]{:S(2)}) copy-start(bf16[1,512,384]{2,1,0:T(8,128)(2,1)} %param.15) | copy-start | bytes 1179652
  3.0 28.7 %all-to-all-start = ((bf16[1,512,3,128]{3,2,0,1:T(4,128)(2,1)}), bf16[1,512,3,128]{3,2,0,1:T(4,128)(2,1)S(1)}, u32[]{:S(2)}, u32[]{:S(2)}) async-start(bf16[1,512,3,128]{3,2,0,1:T(4,128)(2,1)} %copy.94), calls=%async_computation | async-start | bytes 1048576 | tf_op jit(solution)/shard_map/all_to_all | solution.py:157
  15.7 42.6 %copy-start.1 = (bf16[1,512,384]{2,1,0:T(8,128)(2,1)S(1)}, bf16[1,512,384]{2,1,0:T(8,128)(2,1)}, u32[]{:S(2)}) copy-start(bf16[1,512,384]{2,1,0:T(8,128)(2,1)} %param.14) | copy-start | bytes 1179652
  31.6 21.6 %all-to-all-start.1 = ((bf16[1,512,3,128]{3,2,0,1:T(4,128)(2,1)}), bf16[1,512,3,128]{3,2,0,1:T(4,128)(2,1)S(1)}, u32[]{:S(2)}, u32[]{:S(2)}) async-start(bf16[1,512,3,128]{3,2,0,1:T(4,128)(2,1)} %copy.97), calls=%async_computation.1 | async-start | bytes 1048576 | tf_op jit(solution)/shard_map/all_to_all | solution.py:157
  36.9 22.8 %copy-start.46 = (s32[24]{0:T(128)S(1)}, s32[24]{0:T(128)}, u32[]{:S(2)}) copy-start(s32[24]{0:T(128)} %param.17) | copy-start | bytes 292
  53.2 21.4 %all-to-all-start.4 = ((bf16[1,512,3,128]{3,2,0,1:T(4,128)(2,1)}), bf16[1,512,3,128]{3,2,0,1:T(4,128)(2,1)S(1)}, u32[]{:S(2)}, u32[]{:S(2)}) async-start(bf16[1,512,3,128]{3,2,0,1:T(4,128)(2,1)} %copy.109), calls=%async_computation.4 | async-start | bytes 1048576 | tf_op jit(solution)/shard_map/all_to_all | solution.py:157
  74.7 21.4 %all-to-all-start.2 = ((bf16[1,512,3,128]{3,2,0,1:T(4,128)(2,1)}), bf16[1,512,3,128]{3,2,0,1:T(4,128)(2,1)S(1)}, u32[]{:S(2)}, u32[]{:S(2)}) async-start(bf16[1,512,3,128]{3,2,0,1:T(4,128)(2,1)} %copy.102), calls=%async_computation.2 | async-start | bytes 1048576 | tf_op jit(solution)/shard_map/all_to_all | solution.py:157
  96.0 18.7 %all-to-all-start.7 = ((bf16[32,16,3,128]{3,1,2,0:T(8,128)(2,1)}), bf16[32,16,3,128]{3,1,2,0:T(8,128)(2,1)S(1)}, u32[]{:S(2)}, u32[]{:S(2)}) async-start(bf16[32,16,3,128]{3,1,2,0:T(8,128)(2,1)} %copy.123), calls=%async_computation.7 | async-start | bytes 786432 | tf_op jit(solution)/shard_map/all_to_all | solution.py:165
  102.8 16.9 %copy-start.11 = (bf16[32,16,3,128]{3,0,2,1:T(8,128)(2,1)S(1)}, bf16[32,16,3,128]{3,0,2,1:T(8,128)(2,1)}, u32[]{:S(2)}) copy-start(bf16[32,16,3,128]{3,0,2,1:T(8,128)(2,1)} %get-tuple-element.283) | copy-start | bytes 1179652
  102.8 41.9 %copy-start.8 = (bf16[1,512,3,128]{3,1,2,0:T(8,128)(2,1)S(1)}, bf16[1,512,3,128]{3,1,2,0:T(8,128)(2,1)}, u32[]{:S(2)}) copy-start(bf16[1,512,3,128]{3,1,2,0:T(8,128)(2,1)} %copy.95) | copy-start | bytes 1179652
  114.7 32.1 %copy-start.3 = (bf16[32,16,3,128]{3,1,2,0:T(8,128)(2,1)}, bf16[32,16,3,128]{3,1,2,0:T(8,128)(2,1)S(1)}, u32[]{:S(2)}) copy-start(bf16[32,16,3,128]{3,1,2,0:T(8,128)(2,1)S(1)} %all-to-all-done.7) | copy-start | bytes 1179652
  114.7 18.3 %all-to-all-start.5 = ((bf16[32,16,3,128]{3,1,2,0:T(8,128)(2,1)}), bf16[32,16,3,128]{3,1,2,0:T(8,128)(2,1)S(1)}, u32[]{:S(2)}, u32[]{:S(2)}) async-start(bf16[32,16,3,128]{3,1,2,0:T(8,128)(2,1)} %copy.117), calls=%async_computation.5 | async-start | bytes 786432 | tf_op jit(solution)/shard_map/all_to_all | solution.py:163
  119.6 38.3 %copy-start.45 = (s32[24]{0:T(128)S(1)}, s32[24]{0:T(128)}, u32[]{:S(2)}) copy-start(s32[24]{0:T(128)} %param.16) | copy-start | bytes 292
  133.0 37.5 %copy-start.5 = (bf16[32,16,3,128]{3,1,2,0:T(8,128)(2,1)}, bf16[32,16,3,128]{3,1,2,0:T(8,128)(2,1)S(1)}, u32[]{:S(2)}) copy-start(bf16[32,16,3,128]{3,1,2,0:T(8,128)(2,1)S(1)} %all-to-all-done.5) | copy-start | bytes 1179652
  133.0 18.1 %all-to-all-start.3 = ((bf16[32,16,3,128]{3,1,2,0:T(8,128)(2,1)}), bf16[32,16,3,128]{3,1,2,0:T(8,128)(2,1)S(1)}, u32[]{:S(2)}, u32[]{:S(2)}) async-start(bf16[32,16,3,128]{3,1,2,0:T(8,128)(2,1)} %copy.106), calls=%async_computation.3 | async-start | bytes 786432 | tf_op jit(solution)/shard_map/all_to_all | solution.py:162
  137.9 22.7 %collective-permute-start = (bf16[512,384]{1,0:T(8,128)(2,1)S(1)}, bf16[512,384]{1,0:T(8,128)(2,1)}, u32[]{:S(2)}, u32[]{:S(2)}) collective-permute-start(bf16[512,384]{1,0:T(8,128)(2,1)S(1)} %bitcast.64), channel_id=1, source_target_pairs={{0,8},{8,16},{16,24},{24,32},{32,40},{40,48},{48,56},{56,64},{64,7... | collective-permute-start | bytes 1179656 | tf_op jit(solution)/shard_map/ppermute | solution.py:12
  141.3 29.3 %collective-permute-start.1 = (bf16[512,384]{1,0:T(8,128)(2,1)S(1)}, bf16[512,384]{1,0:T(8,128)(2,1)}, u32[]{:S(2)}, u32[]{:S(2)}) collective-permute-start(bf16[512,384]{1,0:T(8,128)(2,1)S(1)} %bitcast.68), channel_id=1, source_target_pairs={{0,8},{8,16},{16,24},{24,32},{32,40},{40,48},{48,56},{56,64},{64,7... | collective-permute-start | bytes 1179656 | tf_op jit(solution)/shard_map/ppermute | solution.py:12
  151.1 19.4 %copy-start.6 = (bf16[32,16,3,128]{3,1,2,0:T(8,128)(2,1)}, bf16[32,16,3,128]{3,1,2,0:T(8,128)(2,1)S(1)}, u32[]{:S(2)}) copy-start(bf16[32,16,3,128]{3,1,2,0:T(8,128)(2,1)S(1)} %all-to-all-done.3) | copy-start | bytes 1179652
  151.1 60.4 %all-to-all-start.6 = ((bf16[32,16,3,128]{3,1,2,0:T(8,128)(2,1)}), bf16[32,16,3,128]{3,1,2,0:T(8,128)(2,1)}, u32[]{:S(2)}, u32[]{:S(2)}) async-start(bf16[32,16,3,128]{3,1,2,0:T(8,128)(2,1)} %copy.120), calls=%async_computation.6 | async-start | bytes 786432 | tf_op jit(solution)/shard_map/all_to_all | solution.py:164
  170.5 10.1 %copy-start.2 = (bf16[1,512,384]{2,1,0:T(8,128)(2,1)S(1)}, bf16[1,512,384]{2,1,0:T(8,128)(2,1)}, u32[]{:S(2)}) copy-start(bf16[1,512,384]{2,1,0:T(8,128)(2,1)} %param.14) | copy-start | bytes 1179652
  201.4 3.8 %copy-start.26 = (bf16[1,512,128]{2,1,0:T(8,128)(2,1)}, bf16[1,512,128]{2,1,0:T(8,128)(2,1)S(1)}, u32[]{:S(2)}) copy-start(bf16[1,512,128]{2,1,0:T(8,128)(2,1)S(1)} %get-tuple-element.163) | copy-start | bytes 393220
  201.4 9.2 %copy-start.7 = (bf16[32,16,3,128]{3,1,2,0:T(8,128)(2,1)S(1)}, bf16[32,16,3,128]{3,1,2,0:T(8,128)(2,1)}, u32[]{:S(2)}) copy-start(bf16[32,16,3,128]{3,1,2,0:T(8,128)(2,1)} %copy-done.6) | copy-start | bytes 1179652
  203.2 10.8 %collective-permute-start.3 = (bf16[512,384]{1,0:T(8,128)(2,1)}, bf16[512,384]{1,0:T(8,128)(2,1)}, u32[]{:S(2)}, u32[]{:S(2)}) collective-permute-start(bf16[512,384]{1,0:T(8,128)(2,1)} %pad_maximum_fusion.19), channel_id=1, source_target_pairs={{8,0},{16,8},{24,16},{32,24},{40,32},{48,40},{56,48},{64,56},{72,6... | collective-permute-start | bytes 1179656 | tf_op jit(solution)/shard_map/ppermute | solution.py:12
  205.2 6.1 %copy-start.4 = (bf16[32,16,3,128]{3,1,2,0:T(8,128)(2,1)S(1)}, bf16[32,16,3,128]{3,1,2,0:T(8,128)(2,1)}, u32[]{:S(2)}) copy-start(bf16[32,16,3,128]{3,1,2,0:T(8,128)(2,1)} %copy-done.3) | copy-start | bytes 1179652
  207.0 10.4 %collective-permute-start.2 = (bf16[512,384]{1,0:T(8,128)(2,1)}, bf16[512,384]{1,0:T(8,128)(2,1)}, u32[]{:S(2)}, u32[]{:S(2)}) collective-permute-start(bf16[512,384]{1,0:T(8,128)(2,1)} %pad_maximum_fusion.18), channel_id=1, source_target_pairs={{8,0},{16,8},{24,16},{32,24},{40,32},{48,40},{56,48},{64,56},{72,6... | collective-permute-start | bytes 1179656 | tf_op jit(solution)/shard_map/ppermute | solution.py:12
  210.3 2.6 %copy-start.20 = (bf16[1,512,128]{2,1,0:T(8,128)(2,1)S(1)}, bf16[1,512,128]{2,1,0:T(8,128)(2,1)}, u32[]{:S(2)}) copy-start(bf16[1,512,128]{2,1,0:T(8,128)(2,1)} %get-tuple-element.258) | copy-start | bytes 393220
  210.3 2.6 %copy-start.22 = (bf16[1,512,128]{2,1,0:T(8,128)(2,1)S(1)}, bf16[1,512,128]{2,1,0:T(8,128)(2,1)}, u32[]{:S(2)}) copy-start(bf16[1,512,128]{2,1,0:T(8,128)(2,1)} %copy-done.21) | copy-start | bytes 393220
  211.3 6.2 %copy-start.13 = (f32[512,128]{1,0:T(8,128)S(1)}, f32[512,128]{1,0:T(8,128)}, u32[]{:S(2)}) copy-start(f32[512,128]{1,0:T(8,128)} %copy-done.12) | copy-start | bytes 786436
  211.3 6.1 %copy-start.15 = (f32[512,128]{1,0:T(8,128)S(1)}, f32[512,128]{1,0:T(8,128)}, u32[]{:S(2)}) copy-start(f32[512,128]{1,0:T(8,128)} %copy-done.14) | copy-start | bytes 786436
  211.3 6.1 %copy-start.17 = (f32[512,128]{1,0:T(8,128)S(1)}, f32[512,128]{1,0:T(8,128)}, u32[]{:S(2)}) copy-start(f32[512,128]{1,0:T(8,128)} %copy-done.16) | copy-start | bytes 786436
  211.3 6.1 %copy-start.19 = (f32[512,128]{1,0:T(8,128)S(1)}, f32[512,128]{1,0:T(8,128)}, u32[]{:S(2)}) copy-start(f32[512,128]{1,0:T(8,128)} %copy-done.18) | copy-start | bytes 786436
  (27 other events, 33.8 us)
where the time goes:
time: 217 us; the launch traced here: 220 us
  waiting for transfers between devices  97.9 us (45%)
  starting transfers between devices  59.1 us (27%)
  local copies, waits for them, and re-layouts  30.3 us (14%)
  matrix products  20.1 us (9%)
  other arithmetic  8.71 us (4%)
  between operations  3.18 us (1%)
    all_to_all x4, waiting for transfers between devices, body(): lax.all_to_all(for_sending(local_rows), 'ctx', split_axis=1, concat_axis=...  57.5 us
    all_to_all x4, starting transfers between devices, body(): lax.all_to_all(for_sending(local_rows), 'ctx', split_axis=1, concat_axis=...  26.9 us
    ppermute x4, waiting for transfers between devices, passed_along(): return lax.ppermute(array, axis, pairs)  13.4 us
    all_to_all x1, waiting for transfers between devices, body(): lax.all_to_all(results[1], 'ctx', split_axis=0, concat_axis=1, tiled=True)  12.4 us
    ppermute x4, starting transfers between devices, passed_along(): return lax.ppermute(array, axis, pairs)  10.6 us
    all_to_all x1, waiting for transfers between devices, body(): lax.all_to_all(results[3], 'ctx', split_axis=0, concat_axis=1, tiled=True)  10.3 us
    all_to_all x1, starting transfers between devices, body(): lax.all_to_all(results[2], 'ctx', split_axis=0, concat_axis=1, tiled=True)  6.75 us
    all_to_all x1, starting transfers between devices, body(): lax.all_to_all(results[3], 'ctx', split_axis=0, concat_axis=1, tiled=True)  5.11 us
  transfers between devices with their start and end apart: 12, of which 9 were waited for; matrix products, arithmetic and copies ran while one was open for 23% of the time, Pallas kernels for 0%

commit v1 on v0

v1 whole, which is shorter than its diff:
```python
import functools
import math

import jax
import jax.numpy as jnp
from jax import lax
from jax.experimental import pallas as pl
from jax.experimental.pallas import tpu as pltpu
from jax.sharding import PartitionSpec as P

DH = 128
HEADS = 24
NSPATIAL = 8
NTEMPORAL = 16
MESH = pl.DeviceIdType.MESH
NEG = -1e30
SCALE = DH ** -0.5
LOG2E = math.log2(math.e)

F32 = jnp.float32
BF16 = jnp.bfloat16

CTX = 32
NY = 4
SH = 8
LH = 3
POS = 512
BLK = 64
SUB = 16
ROWS = CTX * SUB

Q, K, V, G = 0, 1, 2, 3
ATT, QG, KG, VG = 0, 1, 2, 3


def dot_t(a, b):
    return lax.dot_general(a, b, (((1,), (1,)), ((), ())), preferred_element_type=F32)


def dot_n(a, b):
    return lax.dot_general(a, b, (((1,), (0,)), ((), ())), preferred_element_type=F32)


def t_dot(a, b):
    return lax.dot_general(a, b, (((0,), (0,)), ((), ())), preferred_element_type=F32)


def await_bytes(ref, sem):
    pltpu.make_async_copy(ref, ref, sem).wait()


def kernel(
    kind_ref, band_ref, q_hbm, k_hbm, v_hbm, g_hbm,
    att_hbm, qg_hbm, kg_hbm, vg_hbm,
    lists, got0, got1, got2, got3, t_send, t_rows, s_send, s_rows, prior, prior_send, prior_back,
    reach, t_weight, t_prob, t_dscore, s_prob, s_dscore, t_out, s_out, back0, back1, back2, back3, home_send,
    f1_send, f1_recv, t_sent, t_recv, s_sent, s_recv, p_sent, p_recv, b_sent, b_recv,
    rt_sent, rs_sent, r_recv, h_sent, h_recv,
):
    c = lax.axis_index("ctx")
    h = lax.axis_index("head")
    z = lax.div(c, NY)
    inputs = (q_hbm, k_hbm, v_hbm, g_hbm)
    outputs = (att_hbm, qg_hbm, kg_hbm, vg_hbm)
    gathered = (got0, got1, got2, got3)
    results = (back0, back1, back2, back3)

    def ctx_peer(d):
        return lax.rem(c + d, CTX)

    def head_peer(d):
        return lax.rem(h + d, SH)

    def remote(src, dst, send, recv, ctx, head):
        pltpu.make_async_remote_copy(
            src_ref=src, dst_ref=dst, send_sem=send, recv_sem=recv,
            device_id=(ctx, head), device_id_type=MESH,
        ).start()

    barrier = pltpu.get_barrier_semaphore()

    @pl.loop(1, SH)
    def _(d):
        pl.semaphore_signal(barrier, inc=1, device_id=(c, head_peer(d)), device_id_type=MESH)

    @pl.loop(1, CTX)
    def _(d):
        pl.semaphore_signal(barrier, inc=1, device_id=(ctx_peer(d), h), device_id_type=MESH)

    for a in range(4):
        for i in range(LH):
            pltpu.make_async_copy(
                inputs[a].at[pl.ds(h * BLK, BLK), pl.ds(i * DH, DH)],
                gathered[a].at[LH * h + i], f1_recv.at[a],
            ).start()

    kinds = [kind_ref[i] for i in range(HEADS)]
    so_far, count = [], jnp.int32(0)
    limits = [jnp.int32(0), jnp.int32(0)]
    for i in range(HEADS):
        spatial = kinds[i] == 1
        slot = jnp.where(spatial, NTEMPORAL + i - count, count)
        lists[32 + i] = jnp.minimum(slot, HEADS - 1)
        for e in range(2):
            limits[e] = jnp.where(slot == 2 * z + e, band_ref[i] * SUB, limits[e])
        count = count + jnp.where(spatial, 0, 1)
        so_far.append(count)
    for t in range(NTEMPORAL):
        before = sum((jnp.where(so_far[i] <= t, 1, 0) for i in range(HEADS)), jnp.int32(0))
        lists[t] = jnp.minimum(before, HEADS - 1)
    for s in range(NSPATIAL):
        before = sum((jnp.where(i + 1 - so_far[i] <= s, 1, 0) for i in range(HEADS)), jnp.int32(0))
        lists[NTEMPORAL + s] = jnp.minimum(before, HEADS - 1)

    @pl.loop(0, ROWS // 64)
    def _(b):
        row = lax.broadcasted_iota(jnp.int32, (64, ROWS), 0) + b * 64
        col = lax.broadcasted_iota(jnp.int32, (64, ROWS), 1)
        apart = row - col
        reach[pl.ds(b * 64, 64), :] = jnp.where(
            (apart & (SUB - 1)) == 0, jnp.abs(apart), ROWS * 2
        ).astype(F32)

    pl.semaphore_wait(barrier, SH - 1 + CTX - 1)

    for a in range(4):
        @pl.loop(1, SH)
        def _(d):
            to = head_peer(d)
            for i in range(LH):
                remote(
                    inputs[a].at[pl.ds(to * BLK, BLK), pl.ds(i * DH, DH)],
                    gathered[a].at[LH * h + i], f1_send.at[a], f1_recv.at[a], c, to,
                )

    def block_of(a, slot):
        return gathered[a][lists[slot]]

    def select_and_send(a):
        await_bytes(gathered[a], f1_recv.at[a])
        for pair in range(NTEMPORAL // 2):
            for e in range(2):
                block = block_of(a, 2 * pair + e)
                for y in range(NY):
                    t_send[a, pair * NY + y, e] = block[y * SUB:(y + 1) * SUB]
        pltpu.make_async_copy(t_send.at[a, c], t_rows.at[a, c], t_recv.at[a]).start()

        @pl.loop(1, CTX)
        def _(d):
            to = ctx_peer(d)
            remote(t_send.at[a, to], t_rows.at[a, c], t_sent, t_recv.at[a], to, h)

        for s in range(NSPATIAL):
            s_send[a, s] = block_of(a, NTEMPORAL + s)
        pltpu.make_async_copy(s_send.at[a, h], s_rows.at[a, h], s_recv.at[a]).start()

        @pl.loop(1, SH)
        def _(d):
            to = head_peer(d)
            remote(s_send.at[a, to], s_rows.at[a, h], s_sent, s_recv.at[a], c, to)

    for a in (Q, K, V, G):
        select_and_send(a)

    await_bytes(s_rows.at[K], s_recv.at[K])
    await_bytes(s_rows.at[V], s_recv.at[V])
    remote(s_rows.at[K], prior.at[0], p_sent, p_recv, ctx_peer(1), h)
    remote(s_rows.at[V], prior.at[1], p_sent, p_recv, ctx_peer(1), h)

    def t_block(a, e, first, frames):
        return t_rows[a, pl.ds(first, frames), e].reshape(frames * SUB, DH)

    def t_all(a, e):
        return t_block(a, e, 0, CTX)

    await_bytes(t_rows.at[Q], t_recv.at[Q])
    await_bytes(t_rows.at[K], t_recv.at[K])
    for e in range(2):
        keys = t_all(K, e)
        for part in range(2):
            score = dot_t(t_block(Q, e, part * 16, 16), keys) * (SCALE * LOG2E)
            rows = pl.ds(part * 256, 256)
            score = score + jnp.minimum(limits[e].astype(F32) - reach[rows, :], 0.0) * -NEG
            top = jnp.max(score, axis=-1, keepdims=True)
            weight = jnp.exp2(score - top)
            weight = weight * (1.0 / jnp.sum(weight, axis=-1, keepdims=True))
            t_weight[e, rows, :] = weight
            t_prob[e, rows, :] = weight.astype(BF16)

    await_bytes(s_rows.at[Q], s_recv.at[Q])
    await_bytes(s_rows.at[G], s_recv.at[G])
    await_bytes(prior, p_recv)
    k_own = s_rows[K].reshape(POS, DH)
    v_own = s_rows[V].reshape(POS, DH)
    k_prior = prior[0].reshape(POS, DH)
    v_prior = prior[1].reshape(POS, DH)
    part_rows = 128
    part_blocks = part_rows // BLK

    @pl.loop(0, POS // part_rows)
    def _(part):
        rows = pl.ds(part * part_rows, part_rows)
        blocks = pl.ds(part * part_blocks, part_blocks)
        q = s_rows[Q, blocks].reshape(part_rows, DH)
        g = s_rows[G, blocks].reshape(part_rows, DH)
        old = dot_t(q, k_prior) * (SCALE * LOG2E)
        old = jnp.where(c > 0, old, NEG)
        own = dot_t(q, k_own) * (SCALE * LOG2E)
        top = jnp.maximum(
            jnp.max(old, axis=-1, keepdims=True), jnp.max(own, axis=-1, keepdims=True)
        )
        old = jnp.exp2(old - top)
        own = jnp.exp2(own - top)
        inverse = 1.0 / (
            jnp.sum(old, axis=-1, keepdims=True) + jnp.sum(own, axis=-1, keepdims=True)
        )
        old = old * inverse
        own = own * inverse
        old_prob = old.astype(BF16)
        own_prob = own.astype(BF16)
        s_prob[0, rows, :] = old_prob
        s_prob[1, rows, :] = own_prob
        attended = (dot_n(old_prob, v_prior) + dot_n(own_prob, v_own)).astype(BF16)
        s_out[ATT, blocks] = attended.reshape(part_blocks, NY, SUB, DH)
        delta = jnp.sum(g.astype(F32) * attended.astype(F32), axis=-1, keepdims=True)
        old_ds = (old * (dot_t(g, v_prior) - delta) * SCALE).astype(BF16)
        own_ds = (own * (dot_t(g, v_own) - delta) * SCALE).astype(BF16)
        s_dscore[0, rows, :] = old_ds
        s_dscore[1, rows, :] = own_ds
        qg = (dot_n(old_ds, k_prior) + dot_n(own_ds, k_own)).astype(BF16)
        s_out[QG, blocks] = qg.reshape(part_blocks, NY, SUB, DH)

    q_all = s_rows[Q].reshape(POS, DH)
    g_all = s_rows[G].reshape(POS, DH)
    prior_send[0] = t_dot(s_dscore[0], q_all).astype(BF16)
    prior_send[1] = t_dot(s_prob[0], g_all).astype(BF16)
    remote(prior_send, prior_back, b_sent, b_recv, ctx_peer(CTX - 1), h)

    def send_spatial(o):
        pltpu.make_async_copy(s_out.at[o, h], results[o].at[NTEMPORAL + h], r_recv.at[o]).start()

        @pl.loop(1, SH)
        def _(d):
            to = head_peer(d)
            remote(
                s_out.at[o, to], results[o].at[NTEMPORAL + h], rs_sent, r_recv.at[o], c, to
            )

    send_spatial(ATT)
    send_spatial(QG)

    def send_temporal(o):
        mine = results[o].at[pl.ds(2 * z, 2), lax.rem(c, NY)]
        pltpu.make_async_copy(t_out.at[o, c], mine, r_recv.at[o]).start()

        @pl.loop(1, CTX)
        def _(d):
            to = ctx_peer(d)
            remote(t_out.at[o, to], mine, rt_sent, r_recv.at[o], to, h)

    def put(o, e, value):
        t_out[o, :, e] = value.astype(BF16).reshape(CTX, SUB, DH)

    await_bytes(t_rows.at[V], t_recv.at[V])
    for e in range(2):
        put(ATT, e, dot_n(t_prob[e], t_all(V, e)))
    send_temporal(ATT)

    k_total = t_dot(s_dscore[1], q_all)
    v_total = t_dot(s_prob[1], g_all)
    await_bytes(prior_back, b_recv)
    k_total = (k_total + prior_back[0].astype(F32)).astype(BF16)
    v_total = (v_total + prior_back[1].astype(F32)).astype(BF16)
    s_out[KG] = k_total.reshape(SH, NY, SUB, DH)
    s_out[VG] = v_total.reshape(SH, NY, SUB, DH)
    send_spatial(VG)
    send_spatial(KG)

    await_bytes(t_rows.at[G], t_recv.at[G])
    for e in range(2):
        put(VG, e, t_dot(t_prob[e], t_all(G, e)))
    send_temporal(VG)
    for e in range(2):
        values = t_all(V, e)
        keys = t_all(K, e)
        for part in range(2):
            rows = pl.ds(part * 256, 256)
            g = t_block(G, e, part * 16, 16)
            attended = t_out[ATT, pl.ds(part * 16, 16), e].reshape(256, DH)
            delta = jnp.sum(g.astype(F32) * attended.astype(F32), axis=-1, keepdims=True)
            dscore = t_weight[e, rows, :] * (dot_t(g, values) - delta) * SCALE
            t_dscore[e, rows, :] = dscore.astype(BF16)
        put(QG, e, dot_n(t_dscore[e], keys))
    send_temporal(QG)
    for e in range(2):
        put(KG, e, t_dot(t_dscore[e], t_all(Q, e)))
    send_temporal(KG)

    for o in (ATT, VG, QG, KG):
        await_bytes(results[o], r_recv.at[o])
        for head in range(HEADS):
            block = results[o][lists[32 + head]].reshape(BLK, DH)
            shard, column = divmod(head, LH)
            home_send[o, shard, :, column * DH:(column + 1) * DH] = block
        mine = pl.ds(h * BLK, BLK)
        pltpu.make_async_copy(home_send.at[o, h], outputs[o].at[mine, :], h_recv.at[o]).start()

        @pl.loop(1, SH)
        def _(d):
            to = head_peer(d)
            remote(home_send.at[o, to], outputs[o].at[mine, :], h_sent, h_recv.at[o], c, to)

    for o in range(4):
        await_bytes(outputs[o], h_recv.at[o])
    for a in range(4):
        await_bytes(gathered[a].at[pl.ds(0, HEADS - LH)], f1_send.at[a])
    await_bytes(t_rows.at[:, pl.ds(0, CTX - 1)], t_sent)
    await_bytes(s_rows.at[:, pl.ds(0, SH - 1)], s_sent)
    await_bytes(prior, p_sent)
    await_bytes(prior_send, b_sent)
    await_bytes(t_out.at[:, pl.ds(0, CTX - 1)], rt_sent)
    await_bytes(s_out.at[:, pl.ds(0, SH - 1)], rs_sent)
    await_bytes(home_send.at[:, pl.ds(0, SH - 1)], h_sent)


def body(queries, key_rows, value_rows, out_grad, head_kind, frame_band):
    width = LH * DH
    local = [x.reshape(POS, width) for x in (queries, key_rows, value_rows, out_grad)]
    vmem = pltpu.VMEM
    dma = pltpu.SemaphoreType.DMA
    outs = pl.pallas_call(
        kernel,
        out_shape=[jax.ShapeDtypeStruct((POS, width), BF16)] * 4,
        in_specs=[pl.BlockSpec(memory_space=pltpu.SMEM)] * 2
        + [pl.BlockSpec(memory_space=pl.ANY)] * 4,
        out_specs=[pl.BlockSpec(memory_space=pl.ANY)] * 4,
        scratch_shapes=[
            pltpu.SMEM((64,), jnp.int32),
            *[vmem((HEADS, BLK, DH), BF16)] * 4,
            vmem((4, CTX, 2, SUB, DH), BF16),
            vmem((4, CTX, 2, SUB, DH), BF16),
            vmem((4, SH, BLK, DH), BF16),
            vmem((4, SH, BLK, DH), BF16),
            vmem((2, SH, BLK, DH), BF16),
            vmem((2, POS, DH), BF16),
            vmem((2, POS, DH), BF16),
            vmem((ROWS, ROWS), F32),
            vmem((2, ROWS, ROWS), F32),
            vmem((2, ROWS, ROWS), BF16),
            vmem((2, ROWS, ROWS), BF16),
            vmem((2, POS, POS), BF16),
            vmem((2, POS, POS), BF16),
            vmem((4, CTX, 2, SUB, DH), BF16),
            vmem((4, SH, NY, SUB, DH), BF16),
            *[vmem((HEADS, NY, SUB, DH), BF16)] * 4,
            vmem((4, SH, BLK, width), BF16),
            dma((4,)), dma((4,)), dma, dma((4,)), dma, dma((4,)), dma, dma, dma, dma,
            dma, dma, dma((4,)), dma, dma((4,)),
        ],
        compiler_params=pltpu.CompilerParams(
            collective_id=0, has_side_effects=True, vmem_limit_bytes=56 << 20
        ),
        name="video_attention",
    )(head_kind, frame_band, *local)
    return tuple(x[None] for x in outs)


def solution(mesh):
    rows = P("ctx", None, "head")
    return jax.shard_map(
        body,
        mesh=mesh,
        in_specs=(rows, rows, rows, rows, P(), P()),
        out_specs=(rows, rows, rows, rows),
        check_vma=False,
    )
```

time: 217 us -> 98.9 us (0.46)
  the two profiles are of different devices: /device:TPU:34 before, /device:TPU:1 now
where the time goes in v1:
time: 98.9 us; the launch traced here: 98.7 us
  Pallas kernels  93.2 us (94%)
  local copies, waits for them, and re-layouts  4.85 us (5%)
    pallas_call x1, Pallas kernels, body(): pl.pallas_call(kernel, out_shape=[jax.ShapeDtypeStruct((POS, width), BF16...  93.2 us
    unnamed x10, local copies, waits for them, and re-layouts  4.85 us

profile of v1, /device:TPU:1, one launch (start us, length us, event | category | flops | bytes accessed | tf_op | source)
XLA Modules:
  0.0 98.7 jit_solution(10682994889914724366)
XLA Ops:
  0.6 93.2 %video_attention.1 = (bf16[512,384]{1,0:T(8,128)(2,1)}, bf16[512,384]{1,0:T(8,128)(2,1)}, bf16[512,384]{1,0:T(8,128)(2,1)}, bf16[512,384]{1,0:T(8,128)(2,1)}) custom-call(s32[24]{0:T(128)} %kind_ref.1, s32[24]{0:T(128)} %band_ref.1, bf16[512,384]{1,0:T(8,128)(2,1)} %bitcast.12, bf16[512,384]{1,0:T(8,128)(2,1)} %bitcast.13, bf16[512,384]{1,0:T(8,128)(2,1)} %bitcast.14, ...), custom_call_target="tpu_custom_call" | custom-call | tf_op jit(solution)/shard_map/video_attention/pallas_call | solution.py:331
  93.8 0.0 copy-start.2
  93.8 1.8 %copy.14 = bf16[1,512,384]{2,1,0:T(8,128)(2,1)} copy(bf16[1,512,384]{2,1,0:T(8,128)(2,1)} %bitcast.11) | data formatting | bytes 786432
  95.7 0.0 copy-done.2
  95.7 0.0 copy-start.1
  95.7 0.7 copy.15
  96.4 0.4 copy-done.1
  96.8 0.0 copy-start
  96.8 0.7 copy.16
  97.6 0.4 copy-done
  97.9 0.7 copy.17
Async XLA Ops:
  93.8 1.8 %copy-start.2 = (bf16[512,384]{1,0:T(8,128)(2,1)S(1)}, bf16[512,384]{1,0:T(8,128)(2,1)}, u32[]{:S(2)}) copy-start(bf16[512,384]{1,0:T(8,128)(2,1)} %get-tuple-element.9) | copy-start | bytes 1179652
  95.7 1.1 %copy-start.1 = (bf16[512,384]{1,0:T(8,128)(2,1)S(1)}, bf16[512,384]{1,0:T(8,128)(2,1)}, u32[]{:S(2)}) copy-start(bf16[512,384]{1,0:T(8,128)(2,1)} %get-tuple-element.10) | copy-start | bytes 1179652
  96.8 1.1 %copy-start = (bf16[512,384]{1,0:T(8,128)(2,1)S(1)}, bf16[512,384]{1,0:T(8,128)(2,1)}, u32[]{:S(2)}) copy-start(bf16[512,384]{1,0:T(8,128)(2,1)} %get-tuple-element.11) | copy-start | bytes 1179652

commit v2 on v1

--- a/solution.py
+++ b/solution.py
@@ -55,7 +55,7 @@
     lists, got0, got1, got2, got3, t_send, t_rows, s_send, s_rows, prior, prior_send, prior_back,
     reach, t_weight, t_prob, t_dscore, s_prob, s_dscore, t_out, s_out, back0, back1, back2, back3, home_send,
     f1_send, f1_recv, t_sent, t_recv, s_sent, s_recv, p_sent, p_recv, b_sent, b_recv,
-    rt_sent, rs_sent, r_recv, h_sent, h_recv,
+    rt_sent, rs_sent, r_recv, h_sent, h_recv, row_sem,
 ):
     c = lax.axis_index("ctx")
     h = lax.axis_index("head")
@@ -83,9 +83,20 @@
     def _(d):
         pl.semaphore_signal(barrier, inc=1, device_id=(c, head_peer(d)), device_id_type=MESH)
 
-    @pl.loop(1, CTX)
+    y = lax.rem(c, NY)
+
+    def y_peer(d):
+        return z * NY + lax.rem(y + d, NY)
+
+    @pl.loop(1, CTX // NY)
     def _(d):
-        pl.semaphore_signal(barrier, inc=1, device_id=(ctx_peer(d), h), device_id_type=MESH)
+        pl.semaphore_signal(
+            barrier, inc=1, device_id=(ctx_peer(d * NY), h), device_id_type=MESH
+        )
+
+    @pl.loop(1, NY)
+    def _(d):
+        pl.semaphore_signal(barrier, inc=1, device_id=(y_peer(d), h), device_id_type=MESH)
 
     for a in range(4):
         for i in range(LH):
@@ -121,7 +132,7 @@
             (apart & (SUB - 1)) == 0, jnp.abs(apart), ROWS * 2
         ).astype(F32)
 
-    pl.semaphore_wait(barrier, SH - 1 + CTX - 1)
+    pl.semaphore_wait(barrier, SH - 1 + CTX // NY - 1 + NY - 1)
 
     for a in range(4):
         @pl.loop(1, SH)
@@ -132,6 +143,12 @@
                     inputs[a].at[pl.ds(to * BLK, BLK), pl.ds(i * DH, DH)],
                     gathered[a].at[LH * h + i], f1_send.at[a], f1_recv.at[a], c, to,
                 )
+
+    @pl.loop(1, NY)
+    def _(d):
+        pl.semaphore_signal(row_sem, inc=1, device_id=(y_peer(d), h), device_id_type=MESH)
+
+    pl.semaphore_wait(row_sem, NY - 1)
 
     def block_of(a, slot):
         return gathered[a][lists[slot]]
@@ -159,13 +176,13 @@
             to = head_peer(d)
             remote(s_send.at[a, to], s_rows.at[a, h], s_sent, s_recv.at[a], c, to)
 
-    for a in (Q, K, V, G):
+    for a in (K, V, Q):
         select_and_send(a)
-
     await_bytes(s_rows.at[K], s_recv.at[K])
     await_bytes(s_rows.at[V], s_recv.at[V])
     remote(s_rows.at[K], prior.at[0], p_sent, p_recv, ctx_peer(1), h)
     remote(s_rows.at[V], prior.at[1], p_sent, p_recv, ctx_peer(1), h)
+    select_and_send(G)
 
     def t_block(a, e, first, frames):
         return t_rows[a, pl.ds(first, frames), e].reshape(frames * SUB, DH)
@@ -173,8 +190,20 @@
     def t_all(a, e):
         return t_block(a, e, 0, CTX)
 
+    def send_temporal(o):
+        mine = results[o].at[pl.ds(2 * z, 2), lax.rem(c, NY)]
+        pltpu.make_async_copy(t_out.at[o, c], mine, r_recv.at[o]).start()
+
+        @pl.loop(1, CTX)
+        def _(d):
+            to = ctx_peer(d)
+            remote(t_out.at[o, to], mine, rt_sent, r_recv.at[o], to, h)
+
+    def put(o, e, value):
+        t_out[o, :, e] = value.astype(BF16).reshape(CTX, SUB, DH)
+
+    await_bytes(t_rows.at[K], t_recv.at[K])
     await_bytes(t_rows.at[Q], t_recv.at[Q])
-    await_bytes(t_rows.at[K], t_recv.at[K])
     for e in range(2):
         keys = t_all(K, e)
         for part in range(2):
@@ -186,6 +215,10 @@
             weight = weight * (1.0 / jnp.sum(weight, axis=-1, keepdims=True))
             t_weight[e, rows, :] = weight
             t_prob[e, rows, :] = weight.astype(BF16)
+    await_bytes(t_rows.at[V], t_recv.at[V])
+    for e in range(2):
+        put(ATT, e, dot_n(t_prob[e], t_all(V, e)))
+    send_temporal(ATT)
 
     await_bytes(s_rows.at[Q], s_recv.at[Q])
     await_bytes(s_rows.at[G], s_recv.at[G])
@@ -194,7 +227,7 @@
     v_own = s_rows[V].reshape(POS, DH)
     k_prior = prior[0].reshape(POS, DH)
     v_prior = prior[1].reshape(POS, DH)
-    part_rows = 128
+    part_rows = 256
     part_blocks = part_rows // BLK
 
     @pl.loop(0, POS // part_rows)
@@ -230,52 +263,23 @@
         qg = (dot_n(old_ds, k_prior) + dot_n(own_ds, k_own)).astype(BF16)
         s_out[QG, blocks] = qg.reshape(part_blocks, NY, SUB, DH)
 
+    def send_spatial(o):
+        pltpu.make_async_copy(s_out.at[o, h], results[o].at[NTEMPORAL + h], r_recv.at[o]).start()
+
+        @pl.loop(1, SH)
+        def _(d):
+            to = head_peer(d)
+            remote(
+                s_out.at[o, to], results[o].at[NTEMPORAL + h], rs_sent, r_recv.at[o], c, to
+            )
+
     q_all = s_rows[Q].reshape(POS, DH)
     g_all = s_rows[G].reshape(POS, DH)
     prior_send[0] = t_dot(s_dscore[0], q_all).astype(BF16)
     prior_send[1] = t_dot(s_prob[0], g_all).astype(BF16)
     remote(prior_send, prior_back, b_sent, b_recv, ctx_peer(CTX - 1), h)
-
-    def send_spatial(o):
-        pltpu.make_async_copy(s_out.at[o, h], results[o].at[NTEMPORAL + h], r_recv.at[o]).start()
-
-        @pl.loop(1, SH)
-        def _(d):
-            to = head_peer(d)
-            remote(
-                s_out.at[o, to], results[o].at[NTEMPORAL + h], rs_sent, r_recv.at[o], c, to
-            )
-
     send_spatial(ATT)
     send_spatial(QG)
-
-    def send_temporal(o):
-        mine = results[o].at[pl.ds(2 * z, 2), lax.rem(c, NY)]
-        pltpu.make_async_copy(t_out.at[o, c], mine, r_recv.at[o]).start()
-
-        @pl.loop(1, CTX)
-        def _(d):
-            to = ctx_peer(d)
-            remote(t_out.at[o, to], mine, rt_sent, r_recv.at[o], to, h)
-
-    def put(o, e, value):
-        t_out[o, :, e] = value.astype(BF16).reshape(CTX, SUB, DH)
-
-    await_bytes(t_rows.at[V], t_recv.at[V])
-    for e in range(2):
-        put(ATT, e, dot_n(t_prob[e], t_all(V, e)))
-    send_temporal(ATT)
-
-    k_total = t_dot(s_dscore[1], q_all)
-    v_total = t_dot(s_prob[1], g_all)
-    await_bytes(prior_back, b_recv)
-    k_total = (k_total + prior_back[0].astype(F32)).astype(BF16)
-    v_total = (v_total + prior_back[1].astype(F32)).astype(BF16)
-    s_out[KG] = k_total.reshape(SH, NY, SUB, DH)
-    s_out[VG] = v_total.reshape(SH, NY, SUB, DH)
-    send_spatial(VG)
-    send_spatial(KG)
-
     await_bytes(t_rows.at[G], t_recv.at[G])
     for e in range(2):
         put(VG, e, t_dot(t_prob[e], t_all(G, e)))
@@ -296,6 +300,16 @@
         put(KG, e, t_dot(t_dscore[e], t_all(Q, e)))
     send_temporal(KG)
 
+    k_total = t_dot(s_dscore[1], q_all)
+    v_total = t_dot(s_prob[1], g_all)
+    await_bytes(prior_back, b_recv)
+    k_total = (k_total + prior_back[0].astype(F32)).astype(BF16)
+    v_total = (v_total + prior_back[1].astype(F32)).astype(BF16)
+    s_out[KG] = k_total.reshape(SH, NY, SUB, DH)
+    s_out[VG] = v_total.reshape(SH, NY, SUB, DH)
+    send_spatial(VG)
+    send_spatial(KG)
+
     for o in (ATT, VG, QG, KG):
         await_bytes(results[o], r_recv.at[o])
         for head in range(HEADS):
@@ -321,6 +335,19 @@
     await_bytes(t_out.at[:, pl.ds(0, CTX - 1)], rt_sent)
     await_bytes(s_out.at[:, pl.ds(0, SH - 1)], rs_sent)
     await_bytes(home_send.at[:, pl.ds(0, SH - 1)], h_sent)
+
+
+def copy_kernel(*refs):
+    sources, targets, held, in_sem, out_sem = refs[:4], refs[4:8], refs[8], refs[9], refs[10]
+    reads = [pltpu.make_async_copy(x, held.at[o], in_sem.at[o]) for o, x in enumerate(sources)]
+    writes = [pltpu.make_async_copy(held.at[o], x, out_sem.at[o]) for o, x in enumerate(targets)]
+    for read in reads:
+        read.start()
+    for read, write in zip(reads, writes):
+        read.wait()
+        write.start()
+    for write in writes:
+        write.wait()
 
 
 def body(queries, key_rows, value_rows, out_grad, head_kind, frame_band):
@@ -355,13 +382,22 @@
             *[vmem((HEADS, NY, SUB, DH), BF16)] * 4,
             vmem((4, SH, BLK, width), BF16),
             dma((4,)), dma((4,)), dma, dma((4,)), dma, dma((4,)), dma, dma, dma, dma,
-            dma, dma, dma((4,)), dma, dma((4,)),
+            dma, dma, dma((4,)), dma, dma((4,)), pltpu.SemaphoreType.REGULAR,
         ],
         compiler_params=pltpu.CompilerParams(
             collective_id=0, has_side_effects=True, vmem_limit_bytes=56 << 20
         ),
         name="video_attention",
     )(head_kind, frame_band, *local)
+    outs = pl.pallas_call(
+        copy_kernel,
+        out_shape=[jax.ShapeDtypeStruct((POS, width), BF16)] * 4,
+        in_specs=[pl.BlockSpec(memory_space=pl.ANY)] * 4,
+        out_specs=[pl.BlockSpec(memory_space=pl.ANY)] * 4,
+        scratch_shapes=[vmem((4, POS, width), BF16), dma((4,)), dma((4,))],
+        compiler_params=pltpu.CompilerParams(vmem_limit_bytes=56 << 20),
+        name="copy_results",
+    )(*outs)
     return tuple(x[None] for x in outs)
 
 

time: 98.9 us -> 89 us (0.90)
  Pallas kernels: 93.2 us -> 88.3 us
  local copies, waits for them, and re-layouts: 4.85 us -> 0 us
    pallas_call x1, Pallas kernels: 93.2 us -> 86.1 us  [body(): pl.pallas_call(kernel, out_shape=[jax.ShapeDtypeStruct((POS, width), BF16...]
    unnamed x10 -> x0, local copies, waits for them, and re-layouts: 4.85 us -> none
    pallas_call x0 -> x1, Pallas kernels: none -> 2.2 us  [body(): pl.pallas_call(copy_kernel, out_shape=[jax.ShapeDtypeStruct((POS, width),...]
where the time goes in v2:
time: 89 us; the launch traced here: 88.9 us
  Pallas kernels  88.3 us (99%)
    pallas_call x1, Pallas kernels, body(): pl.pallas_call(kernel, out_shape=[jax.ShapeDtypeStruct((POS, width), BF16...  86.1 us
    pallas_call x1, Pallas kernels, body(): pl.pallas_call(copy_kernel, out_shape=[jax.ShapeDtypeStruct((POS, width),...  2.2 us

profile of v2, /device:TPU:1, one launch (start us, length us, event | category | flops | bytes accessed | tf_op | source)
XLA Modules:
  0.0 88.9 jit_solution(12322218417110492501)
XLA Ops:
  0.6 86.1 %video_attention.1 = (bf16[512,384]{1,0:T(8,128)(2,1)}, bf16[512,384]{1,0:T(8,128)(2,1)}, bf16[512,384]{1,0:T(8,128)(2,1)}, bf16[512,384]{1,0:T(8,128)(2,1)}) custom-call(s32[24]{0:T(128)} %kind_ref.1, s32[24]{0:T(128)} %band_ref.1, bf16[512,384]{1,0:T(8,128)(2,1)} %bitcast.8, bf16[512,384]{1,0:T(8,128)(2,1)} %bitcast.9, bf16[512,384]{1,0:T(8,128)(2,1)} %bitcast.10, ...), custom_call_target="tpu_custom_call" | custom-call | tf_op jit(solution)/shard_map/video_attention/pallas_call | solution.py:358
  86.7 2.2 %copy_results.1 = (bf16[512,384]{1,0:T(8,128)(2,1)}, bf16[512,384]{1,0:T(8,128)(2,1)}, bf16[512,384]{1,0:T(8,128)(2,1)}, bf16[512,384]{1,0:T(8,128)(2,1)}) custom-call(bf16[512,384]{1,0:T(8,128)(2,1)} %get-tuple-element.12.refs_0_, bf16[512,384]{1,0:T(8,128)(2,1)} %get-tuple-element.13.refs_1_, bf16[512,384]{1,0:T(8,128)(2,1)} %get-tuple-element.14.refs_2_, ...), custom_call_target="tpu_custom_call" | custom-call | tf_op jit(solution)/shard_map/copy_results/pallas_call | solution.py:392

commit v3 on v2

--- a/solution.py
+++ b/solution.py
@@ -31,6 +31,7 @@
 
 Q, K, V, G = 0, 1, 2, 3
 ATT, QG, KG, VG = 0, 1, 2, 3
+CHUNKS = ((K, 0, 32), (K, 32, 32), (V, 0, 64), (Q, 0, 64), (G, 0, 64))
 
 
 def dot_t(a, b):
@@ -52,17 +53,17 @@
 def kernel(
     kind_ref, band_ref, q_hbm, k_hbm, v_hbm, g_hbm,
     att_hbm, qg_hbm, kg_hbm, vg_hbm,
-    lists, got0, got1, got2, got3, t_send, t_rows, s_send, s_rows, prior, prior_send, prior_back,
+    lists, got0, got1, got2, got3, got4, t_send, t_rows, s_send, s_rows, prior, prior_send, prior_back, relay_up, relay_down,
     reach, t_weight, t_prob, t_dscore, s_prob, s_dscore, t_out, s_out, back0, back1, back2, back3, home_send,
     f1_send, f1_recv, t_sent, t_recv, s_sent, s_recv, p_sent, p_recv, b_sent, b_recv,
-    rt_sent, rs_sent, r_recv, h_sent, h_recv, row_sem,
+    rt_sent, rs_sent, r_recv, h_sent, h_recv, up_sent, up_recv, down_sent, down_recv, row_sem,
 ):
     c = lax.axis_index("ctx")
     h = lax.axis_index("head")
     z = lax.div(c, NY)
     inputs = (q_hbm, k_hbm, v_hbm, g_hbm)
     outputs = (att_hbm, qg_hbm, kg_hbm, vg_hbm)
-    gathered = (got0, got1, got2, got3)
+    gathered = (got0, got1, got2, got3, got4)
     results = (back0, back1, back2, back3)
 
     def ctx_peer(d):
@@ -98,11 +99,14 @@
     def _(d):
         pl.semaphore_signal(barrier, inc=1, device_id=(y_peer(d), h), device_id_type=MESH)
 
-    for a in range(4):
+    def piece(n, shard, i):
+        a, first, count = CHUNKS[n]
+        return inputs[a].at[pl.ds(shard * BLK + first, count), pl.ds(i * DH, DH)]
+
+    for n in range(len(CHUNKS)):
         for i in range(LH):
             pltpu.make_async_copy(
-                inputs[a].at[pl.ds(h * BLK, BLK), pl.ds(i * DH, DH)],
-                gathered[a].at[LH * h + i], f1_recv.at[a],
+                piece(n, h, i), gathered[n].at[LH * h + i], f1_recv.at[n]
             ).start()
 
     kinds = [kind_ref[i] for i in range(HEADS)]
@@ -134,14 +138,14 @@
 
     pl.semaphore_wait(barrier, SH - 1 + CTX // NY - 1 + NY - 1)
 
-    for a in range(4):
+    for n in range(len(CHUNKS)):
         @pl.loop(1, SH)
         def _(d):
             to = head_peer(d)
             for i in range(LH):
                 remote(
-                    inputs[a].at[pl.ds(to * BLK, BLK), pl.ds(i * DH, DH)],
-                    gathered[a].at[LH * h + i], f1_send.at[a], f1_recv.at[a], c, to,
+                    piece(n, to, i), gathered[n].at[LH * h + i],
+                    f1_send.at[n], f1_recv.at[n], c, to,
                 )
 
     @pl.loop(1, NY)
@@ -150,39 +154,63 @@
 
     pl.semaphore_wait(row_sem, NY - 1)
 
-    def block_of(a, slot):
-        return gathered[a][lists[slot]]
-
-    def select_and_send(a):
-        await_bytes(gathered[a], f1_recv.at[a])
+    def select_and_send(n):
+        a, first, count = CHUNKS[n]
+        subs = range(first // SUB, (first + count) // SUB)
+        await_bytes(gathered[n], f1_recv.at[n])
         for pair in range(NTEMPORAL // 2):
             for e in range(2):
-                block = block_of(a, 2 * pair + e)
-                for y in range(NY):
-                    t_send[a, pair * NY + y, e] = block[y * SUB:(y + 1) * SUB]
-        pltpu.make_async_copy(t_send.at[a, c], t_rows.at[a, c], t_recv.at[a]).start()
-
-        @pl.loop(1, CTX)
+                block = gathered[n][lists[2 * pair + e]]
+                for at, sub in enumerate(subs):
+                    t_send[a, pair * NY + sub, e] = block[at * SUB:(at + 1) * SUB]
+
+        @pl.loop(0, CTX // NY)
         def _(d):
-            to = ctx_peer(d)
-            remote(t_send.at[a, to], t_rows.at[a, c], t_sent, t_recv.at[a], to, h)
+            for sub in subs:
+                to = lax.rem(z + d, CTX // NY) * NY + sub
+
+                @pl.when(to == c)
+                def _():
+                    pltpu.make_async_copy(t_send.at[a, c], t_rows.at[a, c], t_recv.at[a]).start()
+
+                @pl.when(to != c)
+                def _():
+                    remote(t_send.at[a, to], t_rows.at[a, c], t_sent, t_recv.at[a], to, h)
 
         for s in range(NSPATIAL):
-            s_send[a, s] = block_of(a, NTEMPORAL + s)
-        pltpu.make_async_copy(s_send.at[a, h], s_rows.at[a, h], s_recv.at[a]).start()
-
-        @pl.loop(1, SH)
-        def _(d):
-            to = head_peer(d)
-            remote(s_send.at[a, to], s_rows.at[a, h], s_sent, s_recv.at[a], c, to)
-
-    for a in (K, V, Q):
-        select_and_send(a)
+            s_send[a, s, pl.ds(first, count)] = gathered[n][lists[NTEMPORAL + s]]
+        if first + count == BLK:
+            pltpu.make_async_copy(s_send.at[a, h], s_rows.at[a, h], s_recv.at[a]).start()
+
+            @pl.loop(1, SH)
+            def _(d):
+                to = head_peer(d)
+                remote(s_send.at[a, to], s_rows.at[a, h], s_sent, s_recv.at[a], c, to)
+
+    for n in range(len(CHUNKS) - 1):
+        select_and_send(n)
     await_bytes(s_rows.at[K], s_recv.at[K])
     await_bytes(s_rows.at[V], s_recv.at[V])
-    remote(s_rows.at[K], prior.at[0], p_sent, p_recv, ctx_peer(1), h)
-    remote(s_rows.at[V], prior.at[1], p_sent, p_recv, ctx_peer(1), h)
-    select_and_send(G)
+    pairs = [pl.ds(2 * r, 2) for r in range(NY)]
+
+    @pl.when(y < NY - 1)
+    def _():
+        remote(s_rows.at[pl.ds(K, 2)], prior, p_sent, p_recv, ctx_peer(1), h)
+
+    @pl.when(y == NY - 1)
+    def _():
+        for r in range(NY - 1):
+            remote(s_rows.at[pl.ds(K, 2), pairs[r]], relay_up, p_sent, up_recv, z * NY + r, h)
+        last = pairs[NY - 1]
+        remote(s_rows.at[pl.ds(K, 2), last], prior.at[:, last], p_sent, p_recv, ctx_peer(1), h)
+
+    select_and_send(len(CHUNKS) - 1)
+
+    @pl.when(y < NY - 1)
+    def _():
+        await_bytes(relay_up, up_recv)
+        above = lax.rem(z + 1, CTX // NY) * NY
+        remote(relay_up, prior.at[:, pl.ds(2 * y, 2)], up_sent, p_recv, above, h)
 
     def t_block(a, e, first, frames):
         return t_rows[a, pl.ds(first, frames), e].reshape(frames * SUB, DH)
@@ -275,15 +303,23 @@
 
     q_all = s_rows[Q].reshape(POS, DH)
     g_all = s_rows[G].reshape(POS, DH)
-    prior_send[0] = t_dot(s_dscore[0], q_all).astype(BF16)
-    prior_send[1] = t_dot(s_prob[0], g_all).astype(BF16)
-    remote(prior_send, prior_back, b_sent, b_recv, ctx_peer(CTX - 1), h)
+    prior_send[0] = t_dot(s_dscore[0], q_all).astype(BF16).reshape(SH, BLK, DH)
+    prior_send[1] = t_dot(s_prob[0], g_all).astype(BF16).reshape(SH, BLK, DH)
+
+    @pl.when(y > 0)
+    def _():
+        remote(prior_send, prior_back, b_sent, b_recv, ctx_peer(CTX - 1), h)
+
+    @pl.when(y == 0)
+    def _():
+        own = pairs[0]
+        remote(prior_send.at[:, own], prior_back.at[:, own], b_sent, b_recv, ctx_peer(CTX - 1), h)
+        for r in range(1, NY):
+            remote(prior_send.at[:, pairs[r]], relay_down, b_sent, down_recv, z * NY + r, h)
+
     send_spatial(ATT)
     send_spatial(QG)
     await_bytes(t_rows.at[G], t_recv.at[G])
-    for e in range(2):
-        put(VG, e, t_dot(t_prob[e], t_all(G, e)))
-    send_temporal(VG)
     for e in range(2):
         values = t_all(V, e)
         keys = t_all(K, e)
@@ -296,21 +332,17 @@
             t_dscore[e, rows, :] = dscore.astype(BF16)
         put(QG, e, dot_n(t_dscore[e], keys))
     send_temporal(QG)
+    @pl.when(y > 0)
+    def _():
+        await_bytes(relay_down, down_recv)
+        below = lax.rem(z + CTX // NY - 1, CTX // NY) * NY + NY - 1
+        remote(relay_down, prior_back.at[:, pl.ds(2 * y, 2)], down_sent, b_recv, below, h)
+
     for e in range(2):
-        put(KG, e, t_dot(t_dscore[e], t_all(Q, e)))
-    send_temporal(KG)
-
-    k_total = t_dot(s_dscore[1], q_all)
-    v_total = t_dot(s_prob[1], g_all)
-    await_bytes(prior_back, b_recv)
-    k_total = (k_total + prior_back[0].astype(F32)).astype(BF16)
-    v_total = (v_total + prior_back[1].astype(F32)).astype(BF16)
-    s_out[KG] = k_total.reshape(SH, NY, SUB, DH)
-    s_out[VG] = v_total.reshape(SH, NY, SUB, DH)
-    send_spatial(VG)
-    send_spatial(KG)
-
-    for o in (ATT, VG, QG, KG):
+        put(VG, e, t_dot(t_prob[e], t_all(G, e)))
+    send_temporal(VG)
+
+    def send_home(o):
         await_bytes(results[o], r_recv.at[o])
         for head in range(HEADS):
             block = results[o][lists[32 + head]].reshape(BLK, DH)
@@ -324,14 +356,42 @@
             to = head_peer(d)
             remote(home_send.at[o, to], outputs[o].at[mine, :], h_sent, h_recv.at[o], c, to)
 
+    for e in range(2):
+        put(KG, e, t_dot(t_dscore[e], t_all(Q, e)))
+    send_home(ATT)
+    send_temporal(KG)
+
+    send_home(QG)
+    k_total = t_dot(s_dscore[1], q_all)
+    v_total = t_dot(s_prob[1], g_all)
+    await_bytes(prior_back, b_recv)
+    k_total = (k_total + prior_back[0].reshape(POS, DH).astype(F32)).astype(BF16)
+    v_total = (v_total + prior_back[1].reshape(POS, DH).astype(F32)).astype(BF16)
+    s_out[KG] = k_total.reshape(SH, NY, SUB, DH)
+    s_out[VG] = v_total.reshape(SH, NY, SUB, DH)
+    send_spatial(VG)
+    send_spatial(KG)
+
+    send_home(VG)
+    send_home(KG)
+
     for o in range(4):
         await_bytes(outputs[o], h_recv.at[o])
-    for a in range(4):
-        await_bytes(gathered[a].at[pl.ds(0, HEADS - LH)], f1_send.at[a])
+    for n in range(len(CHUNKS)):
+        await_bytes(gathered[n].at[pl.ds(0, HEADS - LH)], f1_send.at[n])
     await_bytes(t_rows.at[:, pl.ds(0, CTX - 1)], t_sent)
     await_bytes(s_rows.at[:, pl.ds(0, SH - 1)], s_sent)
     await_bytes(prior, p_sent)
     await_bytes(prior_send, b_sent)
+
+    @pl.when(y < NY - 1)
+    def _():
+        await_bytes(relay_up, up_sent)
+
+    @pl.when(y > 0)
+    def _():
+        await_bytes(relay_down, down_sent)
+
     await_bytes(t_out.at[:, pl.ds(0, CTX - 1)], rt_sent)
     await_bytes(s_out.at[:, pl.ds(0, SH - 1)], rs_sent)
     await_bytes(home_send.at[:, pl.ds(0, SH - 1)], h_sent)
@@ -363,14 +423,16 @@
         out_specs=[pl.BlockSpec(memory_space=pl.ANY)] * 4,
         scratch_shapes=[
             pltpu.SMEM((64,), jnp.int32),
-            *[vmem((HEADS, BLK, DH), BF16)] * 4,
+            *[vmem((HEADS, count, DH), BF16) for _, _, count in CHUNKS],
             vmem((4, CTX, 2, SUB, DH), BF16),
             vmem((4, CTX, 2, SUB, DH), BF16),
             vmem((4, SH, BLK, DH), BF16),
             vmem((4, SH, BLK, DH), BF16),
             vmem((2, SH, BLK, DH), BF16),
-            vmem((2, POS, DH), BF16),
-            vmem((2, POS, DH), BF16),
+            vmem((2, SH, BLK, DH), BF16),
+            vmem((2, SH, BLK, DH), BF16),
+            vmem((2, 2, BLK, DH), BF16),
+            vmem((2, 2, BLK, DH), BF16),
             vmem((ROWS, ROWS), F32),
             vmem((2, ROWS, ROWS), F32),
             vmem((2, ROWS, ROWS), BF16),
@@ -381,8 +443,9 @@
             vmem((4, SH, NY, SUB, DH), BF16),
             *[vmem((HEADS, NY, SUB, DH), BF16)] * 4,
             vmem((4, SH, BLK, width), BF16),
-            dma((4,)), dma((4,)), dma, dma((4,)), dma, dma((4,)), dma, dma, dma, dma,
-            dma, dma, dma((4,)), dma, dma((4,)), pltpu.SemaphoreType.REGULAR,
+            dma((len(CHUNKS),)), dma((len(CHUNKS),)),
+            dma, dma((4,)), dma, dma((4,)), dma, dma, dma, dma,
+            dma, dma, dma((4,)), dma, dma((4,)), dma, dma, dma, dma, pltpu.SemaphoreType.REGULAR,
         ],
         compiler_params=pltpu.CompilerParams(
             collective_id=0, has_side_effects=True, vmem_limit_bytes=56 << 20

time: 89 us -> 83 us (0.933)
  Pallas kernels: 88.3 us -> 81.8 us
    pallas_call x1, Pallas kernels: 86.1 us -> 79.6 us  [body(): pl.pallas_call(kernel, out_shape=[jax.ShapeDtypeStruct((POS, width), BF16...]
where the time goes in v3:
time: 83 us; the launch traced here: 82.5 us
  Pallas kernels  81.8 us (99%)
    pallas_call x1, Pallas kernels, body(): pl.pallas_call(kernel, out_shape=[jax.ShapeDtypeStruct((POS, width), BF16...  79.6 us
    pallas_call x1, Pallas kernels, body(): pl.pallas_call(copy_kernel, out_shape=[jax.ShapeDtypeStruct((POS, width),...  2.2 us

profile of v3, /device:TPU:1, one launch (start us, length us, event | category | flops | bytes accessed | tf_op | source)
XLA Modules:
  0.0 82.5 jit_solution(10064126004538076891)
XLA Ops:
  0.6 79.6 %video_attention.1 = (bf16[512,384]{1,0:T(8,128)(2,1)}, bf16[512,384]{1,0:T(8,128)(2,1)}, bf16[512,384]{1,0:T(8,128)(2,1)}, bf16[512,384]{1,0:T(8,128)(2,1)}) custom-call(s32[24]{0:T(128)} %kind_ref.1, s32[24]{0:T(128)} %band_ref.1, bf16[512,384]{1,0:T(8,128)(2,1)} %bitcast.8, bf16[512,384]{1,0:T(8,128)(2,1)} %bitcast.9, bf16[512,384]{1,0:T(8,128)(2,1)} %bitcast.10, ...), custom_call_target="tpu_custom_call" | custom-call | tf_op jit(solution)/shard_map/video_attention/pallas_call | solution.py:418
  80.3 2.2 %copy_results.1 = (bf16[512,384]{1,0:T(8,128)(2,1)}, bf16[512,384]{1,0:T(8,128)(2,1)}, bf16[512,384]{1,0:T(8,128)(2,1)}, bf16[512,384]{1,0:T(8,128)(2,1)}) custom-call(bf16[512,384]{1,0:T(8,128)(2,1)} %get-tuple-element.12.refs_0_, bf16[512,384]{1,0:T(8,128)(2,1)} %get-tuple-element.13.refs_1_, bf16[512,384]{1,0:T(8,128)(2,1)} %get-tuple-element.14.refs_2_, ...), custom_call_target="tpu_custom_call" | custom-call | tf_op jit(solution)/shard_map/copy_results/pallas_call | solution.py:455

commit v4 on v3

--- a/solution.py
+++ b/solution.py
@@ -31,6 +31,7 @@
 
 Q, K, V, G = 0, 1, 2, 3
 ATT, QG, KG, VG = 0, 1, 2, 3
+Z_ORDER = (4, 3, 5, 2, 6, 1, 7, 0)
 CHUNKS = ((K, 0, 32), (K, 32, 32), (V, 0, 64), (Q, 0, 64), (G, 0, 64))
 
 
@@ -53,10 +54,10 @@
 def kernel(
     kind_ref, band_ref, q_hbm, k_hbm, v_hbm, g_hbm,
     att_hbm, qg_hbm, kg_hbm, vg_hbm,
-    lists, got0, got1, got2, got3, got4, t_send, t_rows, s_send, s_rows, prior, prior_send, prior_back, relay_up, relay_down,
+    lists, got0, got1, got2, got3, got4, t_send, t_rows, s_send, s_rows, prior, prior_send, k_back, v_back, relay_up, relay_down,
     reach, t_weight, t_prob, t_dscore, s_prob, s_dscore, t_out, s_out, back0, back1, back2, back3, home_send,
     f1_send, f1_recv, t_sent, t_recv, s_sent, s_recv, p_sent, p_recv, b_sent, b_recv,
-    rt_sent, rs_sent, r_recv, h_sent, h_recv, up_sent, up_recv, down_sent, down_recv, row_sem,
+    rt_sent, rs_sent, r_recv, h_sent, h_recv, up_sent, up_recv, down_sent, down_recv, met,
 ):
     c = lax.axis_index("ctx")
     h = lax.axis_index("head")
@@ -89,19 +90,31 @@
     def y_peer(d):
         return z * NY + lax.rem(y + d, NY)
 
-    @pl.loop(1, CTX // NY)
-    def _(d):
-        pl.semaphore_signal(
-            barrier, inc=1, device_id=(ctx_peer(d * NY), h), device_id_type=MESH
-        )
+    def z_peer(d):
+        return lax.rem(c + d * NY + CTX, CTX)
+
+    for d in (1, -1):
+        pl.semaphore_signal(barrier, inc=1, device_id=(z_peer(d), h), device_id_type=MESH)
 
     @pl.loop(1, NY)
     def _(d):
         pl.semaphore_signal(barrier, inc=1, device_id=(y_peer(d), h), device_id_type=MESH)
 
+    pl.semaphore_wait(barrier, SH - 1 + 2 + NY - 1)
+
     def piece(n, shard, i):
         a, first, count = CHUNKS[n]
         return inputs[a].at[pl.ds(shard * BLK + first, count), pl.ds(i * DH, DH)]
+
+    for n in range(len(CHUNKS)):
+        @pl.loop(1, SH)
+        def _(d):
+            to = head_peer(d)
+            for i in range(LH):
+                remote(
+                    piece(n, to, i), gathered[n].at[LH * h + i],
+                    f1_send.at[n], f1_recv.at[n], c, to,
+                )
 
     for n in range(len(CHUNKS)):
         for i in range(LH):
@@ -115,7 +128,9 @@
     for i in range(HEADS):
         spatial = kinds[i] == 1
         slot = jnp.where(spatial, NTEMPORAL + i - count, count)
-        lists[32 + i] = jnp.minimum(slot, HEADS - 1)
+        slot_in = jnp.minimum(slot, HEADS - 1)
+        lists[32 + i] = slot_in
+        lists[64 + i] = jnp.where(spatial, slot_in - NTEMPORAL, NSPATIAL)
         for e in range(2):
             limits[e] = jnp.where(slot == 2 * z + e, band_ref[i] * SUB, limits[e])
         count = count + jnp.where(spatial, 0, 1)
@@ -136,23 +151,18 @@
             (apart & (SUB - 1)) == 0, jnp.abs(apart), ROWS * 2
         ).astype(F32)
 
-    pl.semaphore_wait(barrier, SH - 1 + CTX // NY - 1 + NY - 1)
-
-    for n in range(len(CHUNKS)):
-        @pl.loop(1, SH)
-        def _(d):
-            to = head_peer(d)
-            for i in range(LH):
-                remote(
-                    piece(n, to, i), gathered[n].at[LH * h + i],
-                    f1_send.at[n], f1_recv.at[n], c, to,
-                )
+    for far in (1, 2):
+        for d in (far, -far):
+            pl.semaphore_signal(
+                met.at[far - 1], inc=1, device_id=(z_peer(d), h), device_id_type=MESH
+            )
+        pl.semaphore_wait(met.at[far - 1], 2)
 
     @pl.loop(1, NY)
     def _(d):
-        pl.semaphore_signal(row_sem, inc=1, device_id=(y_peer(d), h), device_id_type=MESH)
-
-    pl.semaphore_wait(row_sem, NY - 1)
+        pl.semaphore_signal(met.at[2], inc=1, device_id=(y_peer(d), h), device_id_type=MESH)
+
+    pl.semaphore_wait(met.at[2], NY - 1)
 
     def select_and_send(n):
         a, first, count = CHUNKS[n]
@@ -164,53 +174,76 @@
                 for at, sub in enumerate(subs):
                     t_send[a, pair * NY + sub, e] = block[at * SUB:(at + 1) * SUB]
 
-        @pl.loop(0, CTX // NY)
-        def _(d):
-            for sub in subs:
-                to = lax.rem(z + d, CTX // NY) * NY + sub
-
-                @pl.when(to == c)
-                def _():
-                    pltpu.make_async_copy(t_send.at[a, c], t_rows.at[a, c], t_recv.at[a]).start()
+        for dz in Z_ORDER:
+            @pl.loop(0, len(subs))
+            def _(k):
+                to = lax.rem(z + dz, CTX // NY) * NY + subs[0] + k
+                if dz == 0:
+                    @pl.when(to == c)
+                    def _():
+                        pltpu.make_async_copy(
+                            t_send.at[a, c], t_rows.at[a, c], t_recv.at[a]
+                        ).start()
 
                 @pl.when(to != c)
                 def _():
                     remote(t_send.at[a, to], t_rows.at[a, c], t_sent, t_recv.at[a], to, h)
 
         for s in range(NSPATIAL):
-            s_send[a, s, pl.ds(first, count)] = gathered[n][lists[NTEMPORAL + s]]
-        if first + count == BLK:
-            pltpu.make_async_copy(s_send.at[a, h], s_rows.at[a, h], s_recv.at[a]).start()
-
-            @pl.loop(1, SH)
-            def _(d):
-                to = head_peer(d)
-                remote(s_send.at[a, to], s_rows.at[a, h], s_sent, s_recv.at[a], c, to)
-
-    for n in range(len(CHUNKS) - 1):
-        select_and_send(n)
-    await_bytes(s_rows.at[K], s_recv.at[K])
-    await_bytes(s_rows.at[V], s_recv.at[V])
-    pairs = [pl.ds(2 * r, 2) for r in range(NY)]
-
-    @pl.when(y < NY - 1)
-    def _():
-        remote(s_rows.at[pl.ds(K, 2)], prior, p_sent, p_recv, ctx_peer(1), h)
-
-    @pl.when(y == NY - 1)
-    def _():
-        for r in range(NY - 1):
-            remote(s_rows.at[pl.ds(K, 2), pairs[r]], relay_up, p_sent, up_recv, z * NY + r, h)
-        last = pairs[NY - 1]
-        remote(s_rows.at[pl.ds(K, 2), last], prior.at[:, last], p_sent, p_recv, ctx_peer(1), h)
-
-    select_and_send(len(CHUNKS) - 1)
-
-    @pl.when(y < NY - 1)
-    def _():
-        await_bytes(relay_up, up_recv)
-        above = lax.rem(z + 1, CTX // NY) * NY
-        remote(relay_up, prior.at[:, pl.ds(2 * y, 2)], up_sent, p_recv, above, h)
+            block = gathered[n][lists[NTEMPORAL + s]]
+            s_send[a, s, pl.ds(subs[0], len(subs))] = block.reshape(len(subs), SUB, DH)
+        if first + count < BLK:
+            return
+        pltpu.make_async_copy(s_send.at[a, h], s_rows.at[a, h], s_recv.at[a]).start()
+
+        @pl.loop(1, SH)
+        def _(d):
+            to = head_peer(d)
+            remote(s_send.at[a, to], s_rows.at[a, h], s_sent, s_recv.at[a], c, to)
+
+    above = lax.rem(z + 1, CTX // NY) * NY
+    below = lax.rem(z + CTX // NY - 1, CTX // NY) * NY + NY - 1
+
+    def send_prior(a):
+        i = a - K
+
+        @pl.when(y < NY - 1)
+        def _():
+            @pl.loop(0, SH)
+            def _(s):
+                remote(s_send.at[a, s], prior.at[i, h], p_sent, p_recv, ctx_peer(1), s)
+
+        @pl.when(y == NY - 1)
+        def _():
+            for r in range(NY - 1):
+                remote(s_send.at[a, :, r], relay_up.at[i], p_sent, up_recv.at[i], z * NY + r, h)
+
+            @pl.loop(0, SH)
+            def _(s):
+                remote(
+                    s_send.at[a, s, NY - 1], prior.at[i, h, NY - 1], p_sent, p_recv, above, s
+                )
+
+    def pass_up(a):
+        i = a - K
+
+        @pl.when(y < NY - 1)
+        def _():
+            await_bytes(relay_up.at[i], up_recv.at[i])
+
+            @pl.loop(0, SH)
+            def _(s):
+                remote(relay_up.at[i, s], prior.at[i, h, y], up_sent, p_recv, above, s)
+
+    select_and_send(0)
+    select_and_send(1)
+    send_prior(K)
+    select_and_send(2)
+    send_prior(V)
+    pass_up(K)
+    select_and_send(3)
+    pass_up(V)
+    select_and_send(4)
 
     def t_block(a, e, first, frames):
         return t_rows[a, pl.ds(first, frames), e].reshape(frames * SUB, DH)
@@ -222,10 +255,11 @@
         mine = results[o].at[pl.ds(2 * z, 2), lax.rem(c, NY)]
         pltpu.make_async_copy(t_out.at[o, c], mine, r_recv.at[o]).start()
 
-        @pl.loop(1, CTX)
-        def _(d):
-            to = ctx_peer(d)
-            remote(t_out.at[o, to], mine, rt_sent, r_recv.at[o], to, h)
+        for dz in Z_ORDER:
+            @pl.loop(0 if dz else 1, NY)
+            def _(k):
+                to = lax.rem(z + dz, CTX // NY) * NY + lax.rem(y + k, NY)
+                remote(t_out.at[o, to], mine, rt_sent, r_recv.at[o], to, h)
 
     def put(o, e, value):
         t_out[o, :, e] = value.astype(BF16).reshape(CTX, SUB, DH)
@@ -248,8 +282,8 @@
         put(ATT, e, dot_n(t_prob[e], t_all(V, e)))
     send_temporal(ATT)
 
-    await_bytes(s_rows.at[Q], s_recv.at[Q])
-    await_bytes(s_rows.at[G], s_recv.at[G])
+    for a in range(4):
+        await_bytes(s_rows.at[a], s_recv.at[a])
     await_bytes(prior, p_recv)
     k_own = s_rows[K].reshape(POS, DH)
     v_own = s_rows[V].reshape(POS, DH)
@@ -303,22 +337,31 @@
 
     q_all = s_rows[Q].reshape(POS, DH)
     g_all = s_rows[G].reshape(POS, DH)
-    prior_send[0] = t_dot(s_dscore[0], q_all).astype(BF16).reshape(SH, BLK, DH)
-    prior_send[1] = t_dot(s_prob[0], g_all).astype(BF16).reshape(SH, BLK, DH)
-
-    @pl.when(y > 0)
-    def _():
-        remote(prior_send, prior_back, b_sent, b_recv, ctx_peer(CTX - 1), h)
-
-    @pl.when(y == 0)
-    def _():
-        own = pairs[0]
-        remote(prior_send.at[:, own], prior_back.at[:, own], b_sent, b_recv, ctx_peer(CTX - 1), h)
-        for r in range(1, NY):
-            remote(prior_send.at[:, pairs[r]], relay_down, b_sent, down_recv, z * NY + r, h)
-
-    send_spatial(ATT)
-    send_spatial(QG)
+    prior_send[0] = t_dot(s_dscore[0], q_all).astype(BF16).reshape(SH, NY, SUB, DH)
+    prior_send[1] = t_dot(s_prob[0], g_all).astype(BF16).reshape(SH, NY, SUB, DH)
+    for i, back in enumerate((k_back, v_back)):
+        @pl.when(y > 0)
+        def _():
+            @pl.loop(0, SH)
+            def _(s):
+                remote(prior_send.at[i, s], back.at[h], b_sent, b_recv.at[i], ctx_peer(CTX - 1), s)
+
+        @pl.when(y == 0)
+        def _():
+            for r in range(1, NY):
+                remote(
+                    prior_send.at[i, :, r], relay_down.at[i], b_sent, down_recv, z * NY + r, h
+                )
+
+            @pl.loop(0, SH)
+            def _(s):
+                remote(prior_send.at[i, s, 0], back.at[h, 0], b_sent, b_recv.at[i], below, s)
+
+    s_out[KG] = t_dot(s_dscore[1], q_all).astype(BF16).reshape(SH, NY, SUB, DH)
+    s_out[VG] = t_dot(s_prob[1], g_all).astype(BF16).reshape(SH, NY, SUB, DH)
+    for o in (ATT, QG, VG, KG):
+        send_spatial(o)
+
     await_bytes(t_rows.at[G], t_recv.at[G])
     for e in range(2):
         values = t_all(V, e)
@@ -335,8 +378,10 @@
     @pl.when(y > 0)
     def _():
         await_bytes(relay_down, down_recv)
-        below = lax.rem(z + CTX // NY - 1, CTX // NY) * NY + NY - 1
-        remote(relay_down, prior_back.at[:, pl.ds(2 * y, 2)], down_sent, b_recv, below, h)
+        for i, back in enumerate((k_back, v_back)):
+            @pl.loop(0, SH)
+            def _(s):
+                remote(relay_down.at[i, s], back.at[h, y], down_sent, b_recv.at[i], below, s)
 
     for e in range(2):
         put(VG, e, t_dot(t_prob[e], t_all(G, e)))
@@ -346,6 +391,9 @@
         await_bytes(results[o], r_recv.at[o])
         for head in range(HEADS):
             block = results[o][lists[32 + head]].reshape(BLK, DH)
+            if o in (KG, VG):
+                back = (k_back if o == KG else v_back)[lists[64 + head]].reshape(BLK, DH)
+                block = (block.astype(F32) + back.astype(F32)).astype(BF16)
             shard, column = divmod(head, LH)
             home_send[o, shard, :, column * DH:(column + 1) * DH] = block
         mine = pl.ds(h * BLK, BLK)
@@ -362,16 +410,10 @@
     send_temporal(KG)
 
     send_home(QG)
-    k_total = t_dot(s_dscore[1], q_all)
-    v_total = t_dot(s_prob[1], g_all)
-    await_bytes(prior_back, b_recv)
-    k_total = (k_total + prior_back[0].reshape(POS, DH).astype(F32)).astype(BF16)
-    v_total = (v_total + prior_back[1].reshape(POS, DH).astype(F32)).astype(BF16)
-    s_out[KG] = k_total.reshape(SH, NY, SUB, DH)
-    s_out[VG] = v_total.reshape(SH, NY, SUB, DH)
-    send_spatial(VG)
-    send_spatial(KG)
-
+    for back in (k_back, v_back):
+        back[NSPATIAL] = jnp.zeros((NY, SUB, DH), BF16)
+    for i, back in enumerate((k_back, v_back)):
+        await_bytes(back.at[pl.ds(0, NSPATIAL)], b_recv.at[i])
     send_home(VG)
     send_home(KG)
 
@@ -398,16 +440,12 @@
 
 
 def copy_kernel(*refs):
-    sources, targets, held, in_sem, out_sem = refs[:4], refs[4:8], refs[8], refs[9], refs[10]
-    reads = [pltpu.make_async_copy(x, held.at[o], in_sem.at[o]) for o, x in enumerate(sources)]
-    writes = [pltpu.make_async_copy(held.at[o], x, out_sem.at[o]) for o, x in enumerate(targets)]
-    for read in reads:
-        read.start()
-    for read, write in zip(reads, writes):
-        read.wait()
-        write.start()
-    for write in writes:
-        write.wait()
+    sources, targets, sem = refs[:4], refs[4:8], refs[8]
+    copies = [pltpu.make_async_copy(x, y, sem.at[o]) for o, (x, y) in enumerate(zip(sources, targets))]
+    for copy in copies:
+        copy.start()
+    for copy in copies:
+        copy.wait()
 
 
 def body(queries, key_rows, value_rows, out_grad, head_kind, frame_band):
@@ -422,17 +460,17 @@
         + [pl.BlockSpec(memory_space=pl.ANY)] * 4,
         out_specs=[pl.BlockSpec(memory_space=pl.ANY)] * 4,
         scratch_shapes=[
-            pltpu.SMEM((64,), jnp.int32),
+            pltpu.SMEM((96,), jnp.int32),
             *[vmem((HEADS, count, DH), BF16) for _, _, count in CHUNKS],
             vmem((4, CTX, 2, SUB, DH), BF16),
             vmem((4, CTX, 2, SUB, DH), BF16),
-            vmem((4, SH, BLK, DH), BF16),
-            vmem((4, SH, BLK, DH), BF16),
-            vmem((2, SH, BLK, DH), BF16),
-            vmem((2, SH, BLK, DH), BF16),
-            vmem((2, SH, BLK, DH), BF16),
-            vmem((2, 2, BLK, DH), BF16),
-            vmem((2, 2, BLK, DH), BF16),
+            vmem((4, SH, NY, SUB, DH), BF16),
+            vmem((4, SH, NY, SUB, DH), BF16),
+            vmem((2, SH, NY, SUB, DH), BF16),
+            vmem((2, SH, NY, SUB, DH), BF16),
+            *[vmem((NSPATIAL + 1, NY, SUB, DH), BF16)] * 2,
+            vmem((2, SH, SUB, DH), BF16),
+            vmem((2, SH, SUB, DH), BF16),
             vmem((ROWS, ROWS), F32),
             vmem((2, ROWS, ROWS), F32),
             vmem((2, ROWS, ROWS), BF16),
@@ -444,21 +482,21 @@
             *[vmem((HEADS, NY, SUB, DH), BF16)] * 4,
             vmem((4, SH, BLK, width), BF16),
             dma((len(CHUNKS),)), dma((len(CHUNKS),)),
-            dma, dma((4,)), dma, dma((4,)), dma, dma, dma, dma,
-            dma, dma, dma((4,)), dma, dma((4,)), dma, dma, dma, dma, pltpu.SemaphoreType.REGULAR,
+            dma, dma((4,)), dma, dma((4,)), dma, dma, dma, dma((2,)),
+            dma, dma, dma((4,)), dma, dma((4,)), dma, dma((2,)), dma, dma, pltpu.SemaphoreType.REGULAR((3,)),
         ],
         compiler_params=pltpu.CompilerParams(
-            collective_id=0, has_side_effects=True, vmem_limit_bytes=56 << 20
+            collective_id=0, has_side_effects=True, vmem_limit_bytes=24 << 20
         ),
         name="video_attention",
-    )(head_kind, frame_band, *local)
+    )(*[pltpu.with_memory_space_constraint(x, pltpu.HBM) for x in (head_kind, frame_band, *local)])
     outs = pl.pallas_call(
         copy_kernel,
         out_shape=[jax.ShapeDtypeStruct((POS, width), BF16)] * 4,
         in_specs=[pl.BlockSpec(memory_space=pl.ANY)] * 4,
-        out_specs=[pl.BlockSpec(memory_space=pl.ANY)] * 4,
-        scratch_shapes=[vmem((4, POS, width), BF16), dma((4,)), dma((4,))],
-        compiler_params=pltpu.CompilerParams(vmem_limit_bytes=56 << 20),
+        out_specs=[pl.BlockSpec(memory_space=pltpu.HBM)] * 4,
+        scratch_shapes=[dma((4,))],
+        compiler_params=pltpu.CompilerParams(vmem_limit_bytes=4 << 20),
         name="copy_results",
     )(*outs)
     return tuple(x[None] for x in outs)

time: 83 us -> 75.4 us (0.908)
  Pallas kernels: 81.8 us -> 74.7 us
    pallas_call x1, Pallas kernels: 79.6 us -> 73.5 us  [body(): pl.pallas_call(kernel, out_shape=[jax.ShapeDtypeStruct((POS, width), BF16...]
    pallas_call x1, Pallas kernels: 2.2 us -> 1.17 us  [body(): pl.pallas_call(copy_kernel, out_shape=[jax.ShapeDtypeStruct((POS, width),...]
where the time goes in v4:
time: 75.4 us; the launch traced here: 75.3 us
  Pallas kernels  74.7 us (99%)
    pallas_call x1, Pallas kernels, body(): pl.pallas_call(kernel, out_shape=[jax.ShapeDtypeStruct((POS, width), BF16...  73.5 us

profile of v4, /device:TPU:1, one launch (start us, length us, event | category | flops | bytes accessed | tf_op | source)
XLA Modules:
  0.0 75.3 jit_solution(8112558244411832628)
XLA Ops:
  0.6 73.5 %video_attention.1 = (bf16[512,384]{1,0:T(8,128)(2,1)S(1)}, bf16[512,384]{1,0:T(8,128)(2,1)S(1)}, bf16[512,384]{1,0:T(8,128)(2,1)S(1)}, bf16[512,384]{1,0:T(8,128)(2,1)S(1)}) custom-call(s32[24]{0:T(128)} %kind_ref.1, s32[24]{0:T(128)} %band_ref.1, bf16[512,384]{1,0:T(8,128)(2,1)} %bitcast.8, bf16[512,384]{1,0:T(8,128)(2,1)} %bitcast.9, ...), custom_call_target="tpu_custom_call" | custom-call | tf_op jit(solution)/shard_map/video_attention/pallas_call | solution.py:456
  74.2 1.2 %copy_results.1 = (bf16[512,384]{1,0:T(8,128)(2,1)}, bf16[512,384]{1,0:T(8,128)(2,1)}, bf16[512,384]{1,0:T(8,128)(2,1)}, bf16[512,384]{1,0:T(8,128)(2,1)}) custom-call(bf16[512,384]{1,0:T(8,128)(2,1)S(1)} %get-tuple-element.12.refs_0_, bf16[512,384]{1,0:T(8,128)(2,1)S(1)} %get-tuple-element.13.refs_1_, bf16[512,384]{1,0:T(8,128)(2,1)S(1)} %get-tuple-element.14.refs_2_, ...), custom_call_target="tpu_custom_call" | custom-call | tf_op jit(solution)/shard_map/copy_results/pallas_call | solution.py:493

commit v5 on v4

--- a/solution.py
+++ b/solution.py
@@ -164,10 +164,12 @@
 
     pl.semaphore_wait(met.at[2], NY - 1)
 
-    def select_and_send(n):
+    def await_chunk(n):
+        await_bytes(gathered[n], f1_recv.at[n])
+
+    def select_temporal(n):
         a, first, count = CHUNKS[n]
         subs = range(first // SUB, (first + count) // SUB)
-        await_bytes(gathered[n], f1_recv.at[n])
         for pair in range(NTEMPORAL // 2):
             for e in range(2):
                 block = gathered[n][lists[2 * pair + e]]
@@ -189,6 +191,9 @@
                 def _():
                     remote(t_send.at[a, to], t_rows.at[a, c], t_sent, t_recv.at[a], to, h)
 
+    def select_spatial(n):
+        a, first, count = CHUNKS[n]
+        subs = range(first // SUB, (first + count) // SUB)
         for s in range(NSPATIAL):
             block = gathered[n][lists[NTEMPORAL + s]]
             s_send[a, s, pl.ds(subs[0], len(subs))] = block.reshape(len(subs), SUB, DH)
@@ -235,15 +240,25 @@
             def _(s):
                 remote(relay_up.at[i, s], prior.at[i, h, y], up_sent, p_recv, above, s)
 
-    select_and_send(0)
-    select_and_send(1)
+    await_chunk(0)
+    select_temporal(0)
+    select_spatial(0)
+    await_chunk(1)
+    select_spatial(1)
     send_prior(K)
-    select_and_send(2)
+    select_temporal(1)
+    await_chunk(2)
+    select_spatial(2)
     send_prior(V)
+    select_temporal(2)
     pass_up(K)
-    select_and_send(3)
+    await_chunk(3)
+    select_temporal(3)
+    select_spatial(3)
     pass_up(V)
-    select_and_send(4)
+    await_chunk(4)
+    select_temporal(4)
+    select_spatial(4)
 
     def t_block(a, e, first, frames):
         return t_rows[a, pl.ds(first, frames), e].reshape(frames * SUB, DH)

time: 75.4 us -> 75.6 us (level)
  no operation moved by 1% of the time
where the time goes in v5:
time: 75.6 us; the launch traced here: 75.5 us
  Pallas kernels  74.9 us (99%)
    pallas_call x1, Pallas kernels, body(): pl.pallas_call(kernel, out_shape=[jax.ShapeDtypeStruct((POS, width), BF16...  73.7 us

profile of v5, /device:TPU:1, one launch (start us, length us, event | category | flops | bytes accessed | tf_op | source)
XLA Modules:
  0.0 75.5 jit_solution(5668477522124478066)
XLA Ops:
  0.6 73.7 %video_attention.1 = (bf16[512,384]{1,0:T(8,128)(2,1)S(1)}, bf16[512,384]{1,0:T(8,128)(2,1)S(1)}, bf16[512,384]{1,0:T(8,128)(2,1)S(1)}, bf16[512,384]{1,0:T(8,128)(2,1)S(1)}) custom-call(s32[24]{0:T(128)} %kind_ref.1, s32[24]{0:T(128)} %band_ref.1, bf16[512,384]{1,0:T(8,128)(2,1)} %bitcast.8, bf16[512,384]{1,0:T(8,128)(2,1)} %bitcast.9, ...), custom_call_target="tpu_custom_call" | custom-call | tf_op jit(solution)/shard_map/video_attention/pallas_call | solution.py:471
  74.3 1.2 %copy_results.1 = (bf16[512,384]{1,0:T(8,128)(2,1)}, bf16[512,384]{1,0:T(8,128)(2,1)}, bf16[512,384]{1,0:T(8,128)(2,1)}, bf16[512,384]{1,0:T(8,128)(2,1)}) custom-call(bf16[512,384]{1,0:T(8,128)(2,1)S(1)} %get-tuple-element.12.refs_0_, bf16[512,384]{1,0:T(8,128)(2,1)S(1)} %get-tuple-element.13.refs_1_, bf16[512,384]{1,0:T(8,128)(2,1)S(1)} %get-tuple-element.14.refs_2_, ...), custom_call_target="tpu_custom_call" | custom-call | tf_op jit(solution)/shard_map/copy_results/pallas_call | solution.py:508
